TPU v7x, 128 devices: a whole 4x4x4 slice. The times are simulated.
128 devices in a mesh: dp: 8 (over z, core), seq: 16 (over x, y).
Axes of the slice: x: 4, y: 4, z: 4, core: 2. Of those that a mesh axis runs over, the one named last changes fastest.
Arguments:
- dec_input: bfloat16 [128, 128, 768], P(('dp', 'seq')), may hold values from -6 to 6
- memory: bfloat16 [128, 3072, 768], P('dp', 'seq'), may hold values from -6 to 6
- mem_len: int32 [128], P(('dp', 'seq')), may hold values from 1 to 3072, 196608 in all
- grad_out: bfloat16 [128, 128, 768], P(('dp', 'seq')), may hold values from -6 to 6
- attn_master: float32 [8, 768, 768], P(None, ('dp', 'seq'))
- ffn_in_master: float32 [2, 768, 2048], P(None, ('dp', 'seq')), may hold values from -0.21875 to 0.21875
- ffn_out_master: float32 [2048, 768], P(('dp', 'seq')), may hold values from -0.125 to 0.125
- gain_master: float32 [3, 768], P(None, ('dp', 'seq')), may hold values from 0.5 to 1.5
- attn_first: float32 [8, 768, 768], P(None, ('dp', 'seq')), may hold values from -64 to 64
- ffn_in_first: float32 [2, 768, 2048], P(None, ('dp', 'seq')), may hold values from -40 to 40
- ffn_out_first: float32 [2048, 768], P(('dp', 'seq')), may hold values from -40 to 40
- gain_first: float32 [3, 768], P(None, ('dp', 'seq')), may hold values from -96 to 96
- attn_second: float32 [8, 768, 768], P(None, ('dp', 'seq'))
- ffn_in_second: float32 [2, 768, 2048], P(None, ('dp', 'seq')), may hold values from 4.096 to 16.384
- ffn_out_second: float32 [2048, 768], P(('dp', 'seq')), may hold values from 4.096 to 16.384
- gain_second: float32 [3, 768], P(None, ('dp', 'seq'))
Outputs:
- out_block: bfloat16 [128, 128, 768], P(('dp', 'seq'))
- grad_input: float32 [128, 128, 768], P(('dp', 'seq'))
- grad_memory: float32 [128, 3072, 768], P('dp', 'seq')
- attn_new: float32 [8, 768, 768], P(None, ('dp', 'seq'))
- attn_first_new: float32 [8, 768, 768], P(None, ('dp', 'seq'))
- attn_second_new: float32 [8, 768, 768], P(None, ('dp', 'seq'))
- attn_copy: bfloat16 [8, 768, 768], P(None, ('dp', 'seq'))
- ffn_in_new: float32 [2, 768, 2048], P(None, ('dp', 'seq'))
- ffn_in_first_new: float32 [2, 768, 2048], P(None, ('dp', 'seq'))
- ffn_in_second_new: float32 [2, 768, 2048], P(None, ('dp', 'seq'))
- ffn_in_copy: bfloat16 [2, 768, 2048], P(None, ('dp', 'seq'))
- ffn_out_new: float32 [2048, 768], P(('dp', 'seq'))
- ffn_out_first_new: float32 [2048, 768], P(('dp', 'seq'))
- ffn_out_second_new: float32 [2048, 768], P(('dp', 'seq'))
- ffn_out_copy: bfloat16 [2048, 768], P(('dp', 'seq'))
- gain_new: float32 [3, 768], P(None, ('dp', 'seq'))
- gain_first_new: float32 [3, 768], P(None, ('dp', 'seq'))
- gain_second_new: float32 [3, 768], P(None, ('dp', 'seq'))
- gain_copy: bfloat16 [3, 768], P(None, ('dp', 'seq'))
Inputs may be any that keep to these rules, and one draw needn't show every extreme that they name: `mem_len`: each example's count of live memory positions; the largest is exactly 3072.
All inputs are finite; a program needn't handle non-finite values. No bound on the sum of `mem_len` on one device may be relied on, other than what follows from the above.
Results may differ from a plain program's by a relative error of at most 0.02.
The roundings to bfloat16 on the way count: a program that leaves them out, or rounds other values in their place, can miss the bound.
Values may be sent and summed in bfloat16 or wider, within the bound.
A program may use at most 256 MiB of HBM per device.

v0:
```python
import jax
import jax.numpy as jnp
from jax import lax
from jax.experimental import pallas as pl
from jax.experimental.pallas import tpu as pltpu
from jax.sharding import PartitionSpec as P

eps_norm = 1e-06
beta_one = 0.9
beta_two = 0.999
adam_eps = 1e-08
decay_rate = 0.01
rate_matrix = 0.12
rate_gain = 3.0
STEP = 10
MESH = pl.DeviceIdType.MESH
BF, F32 = jnp.bfloat16, jnp.float32
ALL = slice(None)
PARTS = (("A", 0, "xyz"), ("A", 1, "yzx"), ("A", 2, "zxy"), ("B", 0, "xyz"), ("B", 1, "yzx"), ("C", 0, "zxy"))

def where_am_i():
    dp, sq = lax.axis_index("dp"), lax.axis_index("seq")
    return {"x": sq // 4, "y": sq % 4, "z": dp // 2, "c": dp % 2}

def dev(at):
    return (at["z"] * 2 + at["c"], at["x"] * 4 + at["y"])

def moved(at, axis, step):
    return {**at, axis: (at[axis] + step + 4) % 4}

def gather_kernel(attn, wi, wo, info, A, B, C, gains, lens, infos, stage, recv, blk, blkA, blkB, blkC, irecv,
                  ss, rs, sib_s, sib_r, as_, ar_, is_, ir_, ds_, dr_, own_s):
    me = where_am_i()
    dp, sq = lax.axis_index("dp"), lax.axis_index("seq")
    bar = pltpu.get_barrier_semaphore()
    for i in range(1, 16):
        pl.semaphore_signal(bar, inc=1, device_id=(dp, (sq + i) % 16), device_id_type=MESH)
    for i in range(1, 8):
        pl.semaphore_signal(bar, inc=1, device_id=((dp + i) % 8, sq), device_id_type=MESH)
    stage[:, 6:8, :] = jnp.zeros((16, 2, 640), F32)
    for s in range(16):
        stage[s, 0:6, 0:384] = attn[:, s // 2, 384 * (s % 2):384 * (s % 2) + 384]
        stage[s, 0:6, 384:640] = wi[:, s // 8, 256 * (s % 8):256 * (s % 8) + 256]
    pl.semaphore_wait(bar, 22)
    def a2a(i):
        peer = (sq + i) % 16
        return pltpu.make_async_remote_copy(stage.at[peer], recv.at[sq], as_.at[i], ar_.at[i], device_id=(dp, peer), device_id_type=MESH)
    def inf(i):
        peer = (sq + i) % 16
        return pltpu.make_async_remote_copy(info, irecv.at[sq], is_.at[i], ir_.at[i], device_id=(dp, peer), device_id_type=MESH)
    for i in range(1, 16):
        a2a(i).start()
    for i in range(1, 16):
        inf(i).start()
    recv[sq] = stage[sq]
    irecv[sq] = info[...]
    blkC[...] = wo[...].astype(BF)
    for i in range(1, 16):
        a2a(i).wait_recv()
    for k in range(16):
        blk[6 * k:6 * k + 6, :] = recv[k, 0:6, :]
    for p in range(3):
        blkA[p] = blk[32 * p:32 * p + 32, 0:384].astype(BF)
    for p in range(2):
        blkB[p] = blk[48 * p:48 * p + 48, 384:640].astype(BF)

    def view(part, at):
        name, p, _ = part
        if name == "A":
            return A.at[at["x"], at["y"], at["z"], at["c"], p]
        if name == "B":
            return B.at[at["x"], at["y"], at["z"], at["c"], p]
        return C.at[at["z"], at["c"], at["x"], at["y"]]

    def mine(part):
        name, p, _ = part
        return blkA.at[p] if name == "A" else blkB.at[p] if name == "B" else blkC

    def group(part, t, step, half=None):
        order = part[2]
        at = moved(me, order[t], step)
        for j in range(t):
            at = {**at, order[j]: ALL}
        if half is not None and t:
            at = {**at, order[0]: pl.ds(2 * half, 2)}
        return at

    def send(n, t, kind):
        part = PARTS[n]
        axis = part[2][t]
        step = 1 if kind in (0, 2) else -1
        if kind < 2:
            dst = view(part, group(part, t, 0))
            src = mine(part) if t == 0 else dst
        else:
            dst = src = view(part, group(part, t, -step, kind - 2))
        return pltpu.make_async_remote_copy(src, dst, ss.at[n, t, kind], rs.at[n, t, kind], device_id=dev(moved(me, axis, step)), device_id_type=MESH)

    def arrival(n, t, kind):
        part = PARTS[n]
        axis = part[2][t]
        step = 1 if kind in (0, 2) else -1
        if kind < 2:
            dst = view(part, group(part, t, -step))
        else:
            dst = view(part, group(part, t, -2 * step, kind - 2))
        return pltpu.make_async_remote_copy(dst, dst, ss.at[n, t, kind], rs.at[n, t, kind], device_id=dev(moved(me, axis, step)), device_id_type=MESH)

    def kinds(n, t):
        return (0, 1, 2, 3) if t else (0, 1, 2 + n % 2)

    def sibling(n, j, c):
        part = PARTS[n]
        steps = (0, -1, 1, 2)
        at = {**group(part, 2, steps[j]), "c": c}
        v = view(part, at)
        return pltpu.make_async_remote_copy(v, v, sib_s.at[n, j], sib_r.at[n, j], device_id=dev({**me, "c": 1 - me["c"]}), device_id_type=MESH)

    owns = [pltpu.make_async_copy(mine(PARTS[n]), view(PARTS[n], me), own_s.at[n]) for n in range(6)]
    for o in owns:
        o.start()
    for t in range(3):
        for n in range(6):
            if t == 1:
                owns[n].wait()
            if t:
                for k in kinds(n, t - 1)[2:]:
                    arrival(n, t - 1, k).wait_recv()
            send(n, t, 0).start()
            send(n, t, 1).start()
            if t == 2:
                sibling(n, 0, me["c"]).start()
        for n in range(6):
            for k in (0, 1):
                arrival(n, t, k).wait_recv()
                if 2 + k in kinds(n, t):
                    send(n, t, 2 + k).start()
                if t == 2:
                    sibling(n, 1 + k, me["c"]).start()
    for i in range(1, 16):
        inf(i).wait_recv()
    tile = jnp.sum(irecv[...], axis=0)
    infos[dp] = tile
    def dpx(i):
        return pltpu.make_async_remote_copy(infos.at[dp], infos.at[dp], ds_.at[i], dr_.at[i], device_id=((dp + i) % 8, sq), device_id_type=MESH)
    def dpx_in(i):
        return pltpu.make_async_remote_copy(infos.at[(dp - i + 8) % 8], infos.at[(dp - i + 8) % 8], ds_.at[i], dr_.at[i], device_id=((dp + i) % 8, sq), device_id_type=MESH)
    for i in range(1, 8):
        dpx(i).start()
    for n in range(6):
        for k in (2, 3):
            arrival(n, 2, k).wait_recv()
        sibling(n, 3, me["c"]).start()
    for i in range(1, 8):
        dpx_in(i).wait_recv()
    lane = lax.broadcasted_iota(jnp.int32, (8, 128), 1)
    gains[...] = jnp.zeros((8, 768), F32)
    for d in range(8):
        lo, sh = 96 * d // 128, 96 * d % 128
        t = pltpu.roll(jnp.where(lane < 96, infos[d], 0.0), sh, 1)
        gains[:, 128 * lo:128 * lo + 128] += jnp.where(lane >= sh, t, 0.0)
        if sh > 32:
            gains[:, 128 * lo + 128:128 * lo + 256] += jnp.where(lane < sh, t, 0.0)
    pick = lax.broadcasted_iota(jnp.int32, (16, 128), 0) == lax.broadcasted_iota(jnp.int32, (16, 128), 1)
    lens[...] = jnp.broadcast_to(jnp.sum(jnp.where(pick, tile[3:4, :], 0.0), axis=1, keepdims=True), (16, 128))
    for n in range(6):
        for j in range(4):
            sibling(n, j, 1 - me["c"]).wait_recv()
    for i in range(1, 16):
        a2a(i).wait_send()
        inf(i).wait_send()
    for i in range(1, 8):
        dpx(i).wait_send()
    for n in range(6):
        for t in range(3):
            for k in kinds(n, t):
                send(n, t, k).wait_send()
        for j in range(4):
            sibling(n, j, me["c"]).wait_send()

def gather(attn, wi, wo, info):
    V = pl.BlockSpec(memory_space=pltpu.VMEM)
    H = pl.BlockSpec(memory_space=pltpu.HBM)
    D = pltpu.SemaphoreType.DMA
    return pl.pallas_call(
        gather_kernel,
        out_shape=(jax.ShapeDtypeStruct((4, 4, 4, 2, 3, 32, 384), BF),
                   jax.ShapeDtypeStruct((4, 4, 4, 2, 2, 48, 256), BF),
                   jax.ShapeDtypeStruct((4, 2, 4, 4, 16, 768), BF),
                   jax.ShapeDtypeStruct((8, 768), F32), jax.ShapeDtypeStruct((16, 128), F32)),
        in_specs=[V] * 4, out_specs=(H, H, H, V, V),
        scratch_shapes=[pltpu.VMEM((8, 8, 128), F32), pltpu.VMEM((16, 8, 640), F32), pltpu.VMEM((16, 8, 640), F32), pltpu.VMEM((96, 640), F32),
                        pltpu.VMEM((3, 32, 384), BF), pltpu.VMEM((2, 48, 256), BF), pltpu.VMEM((16, 768), BF),
                        pltpu.VMEM((16, 8, 128), F32),
                        D((6, 3, 4)), D((6, 3, 4)), D((6, 4)), D((6, 4)), D((16,)), D((16,)), D((16,)), D((16,)), D((8,)), D((8,)), D((6,))],
        compiler_params=pltpu.CompilerParams(collective_id=0, has_side_effects=True, vmem_limit_bytes=60 << 20),
        name="gather_weights",
    )(attn, wi, wo, info)

def info_tile(gain, mem_len):
    sq = lax.axis_index("seq")
    t = jnp.zeros((8, 128), F32)
    t = lax.dynamic_update_slice(t, gain.astype(BF).astype(F32), (0, 6 * sq))
    return lax.dynamic_update_slice(t, mem_len.astype(F32)[:, None], (3, sq))


def scatter_kernel(GA, GB, GC, gg, oA, oB, oC, oG, accA, accB, accC, sibA, sibB, sibC,
                   hA2, hB2, hC2, fA2, fB2, fC2, hA1, hB1, hC1, fA1, fB1, fC1, hA0, hB0, hC0, fA0, fB0, fC0,
                   blk, stage, recv, gdp, gsum, gsq,
                   ss, rs, sib_s, sib_r, loc_s, as_, ar_, is_, ir_, ds_, dr_):
    me = where_am_i()
    dp, sq = lax.axis_index("dp"), lax.axis_index("seq")
    acc = {"A": accA, "B": accB, "C": accC}
    sib = {"A": sibA, "B": sibB, "C": sibC}
    hop = {2: {"A": hA2, "B": hB2, "C": hC2}, 1: {"A": hA1, "B": hB1, "C": hC1}, 0: {"A": hA0, "B": hB0, "C": hC0}}
    fin = {2: {"A": fA2, "B": fB2, "C": fC2}, 1: {"A": fA1, "B": fB1, "C": fC1}, 0: {"A": fA0, "B": fB0, "C": fC0}}
    bar = pltpu.get_barrier_semaphore()
    for i in range(1, 16):
        pl.semaphore_signal(bar, inc=1, device_id=(dp, (sq + i) % 16), device_id_type=MESH)
    for i in range(1, 8):
        pl.semaphore_signal(bar, inc=1, device_id=((dp + i) % 8, sq), device_id_type=MESH)
    pl.semaphore_wait(bar, 22)

    def idx(part, at):
        name, p, _ = part
        if name == "C":
            return (at["z"], at["x"], at["y"])
        return (p, at["x"], at["y"], at["z"])

    def source(part, at, c):
        name, p, _ = part
        if name == "A":
            return GA.at[at["x"], at["y"], at["z"], c, p]
        if name == "B":
            return GB.at[at["x"], at["y"], at["z"], c, p]
        return GC.at[at["z"], c, at["x"], at["y"]]

    def names(part):
        return "zxy" if part[0] == "C" else "xyz"

    def group(part, t, step):
        order = part[2]
        at = moved(me, order[t], step)
        for j in range(t):
            at = {**at, order[j]: ALL}
        return at

    def halved(part, t, at, half):
        if t == 0:
            return at
        first = [a for a in names(part) if a in part[2][:t]][0]
        return {**at, first: pl.ds(2 * half, 2)}

    def done(part, t):
        return [a for a in names(part) if a in part[2][:t]]

    STEPS = (2, -1, 1, 0)
    other = dev({**me, "c": 1 - me["c"]})

    def sib_copy(n, j):
        part = PARTS[n]
        at = group(part, 2, STEPS[j])
        return pltpu.make_async_remote_copy(source(part, at, 1 - me["c"]), sib[part[0]].at[idx(part, at)], sib_s.at[n, j], sib_r.at[n, j], device_id=other, device_id_type=MESH)

    def loc_copy(n, j):
        part = PARTS[n]
        at = group(part, 2, STEPS[j])
        return pltpu.make_async_copy(source(part, at, me["c"]), acc[part[0]].at[idx(part, at)], loc_s.at[n, j])

    def slot(part):
        return () if part[0] == "C" else (part[1],)

    def kinds(n, t):
        return (0, 1) if t else (n % 2,)

    def hop_send(n, t, kind):
        part = PARTS[n]
        step = 1 if kind == 0 else -1
        at = halved(part, t, group(part, t, 2 * step), kind)
        return pltpu.make_async_remote_copy(acc[part[0]].at[idx(part, at)], hop[t][part[0]].at[slot(part) + (kind,)],
                                            ss.at[n, t, kind], rs.at[n, t, kind], device_id=dev(moved(me, part[2][t], step)), device_id_type=MESH)

    def fin_send(n, t, kind):
        part = PARTS[n]
        step = 1 if kind == 0 else -1
        at = group(part, t, step)
        return pltpu.make_async_remote_copy(acc[part[0]].at[idx(part, at)], fin[t][part[0]].at[slot(part) + (kind,)],
                                            ss.at[n, t, 2 + kind], rs.at[n, t, 2 + kind], device_id=dev(moved(me, part[2][t], step)), device_id_type=MESH)

    def each(part, t, at, fn, half=None):
        axes = done(part, t)
        sizes = [4] * len(axes)
        offs = [0] * len(axes)
        if half is not None and axes:
            sizes[0] = 2
            offs[0] = 2 * half
        total = 1
        for s in sizes:
            total *= s
        def one(i):
            pos = []
            rest = i
            for s in sizes[::-1]:
                pos.append(rest % s)
                rest = rest // s
            pos = pos[::-1]
            where = dict(at)
            for a, p, o in zip(axes, pos, offs):
                where[a] = p + o
            fn(idx(part, where), tuple(pos))
        if total == 1:
            one(0)
        else:
            pl.loop(0, total)(one)

    def merge_sibling(n, j):
        part = PARTS[n]
        sib_copy(n, j).wait_recv()
        loc_copy(n, j).wait()
        a, b = acc[part[0]], sib[part[0]]
        def fn(i, _):
            a[i] = (a[i].astype(F32) + b[i].astype(F32)).astype(BF)
        each(part, 2, group(part, 2, STEPS[j]), fn)

    for j in range(4):
        for n in range(6):
            sib_copy(n, j).start()
            loc_copy(n, j).start()
    def dpx(i):
        peer = (dp + i) % 8
        return pltpu.make_async_remote_copy(gg.at[peer], gdp.at[dp], ds_.at[i], dr_.at[i], device_id=(peer, sq), device_id_type=MESH)
    for i in range(1, 8):
        dpx(i).start()
    gdp[dp] = gg[dp]
    for t in (2, 1, 0):
        for n in range(6):
            if t == 2:
                merge_sibling(n, 0)
            else:
                finish(n, t + 1)
            for k in kinds(n, t):
                hop_send(n, t, k).start()
        if t == 2:
            for n in range(6):
                merge_sibling(n, 1)
                merge_sibling(n, 2)
        for n in range(6):
            part = PARTS[n]
            for k in (0, 1):
                if k in kinds(n, t):
                    hop_send(n, t, k).wait_recv()
                    a, b = acc[part[0]], hop[t][part[0]]
                    def fn(i, pos, a=a, b=b, part=part, k=k):
                        j = slot(part) + (k,) + pos
                        a[i] = (a[i].astype(F32) + b[j].astype(F32)).astype(BF)
                    each(part, t, group(part, t, 1 if k == 0 else -1), fn, k)
                fin_send(n, t, k).start()
        if t == 2:
            for n in range(6):
                merge_sibling(n, 3)

        def finish(n, t):
            part = PARTS[n]
            fin_send(n, t, 0).wait_recv()
            fin_send(n, t, 1).wait_recv()
            a, b = acc[part[0]], fin[t][part[0]]
            def fn(i, pos):
                s = slot(part)
                a[i] = (a[i].astype(F32) + b[s + (0,) + pos].astype(F32) + b[s + (1,) + pos].astype(F32)).astype(BF)
            each(part, t, group(part, t, 0), fn)

    for n in range(6):
        part = PARTS[n]
        fin_send(n, 0, 0).wait_recv()
        fin_send(n, 0, 1).wait_recv()
        a, b = acc[part[0]], fin[0][part[0]]
        s = slot(part)
        v = a[idx(part, me)].astype(F32) + b[s + (0,)].astype(F32) + b[s + (1,)].astype(F32)
        if part[0] == "A":
            blk[32 * part[1]:32 * part[1] + 32, 0:384] = v
        elif part[0] == "B":
            blk[48 * part[1]:48 * part[1] + 48, 384:640] = v
        else:
            oC[...] = v
    stage[:, 6:8, :] = jnp.zeros((16, 2, 640), F32)
    for k in range(16):
        stage[k, 0:6, :] = blk[6 * k:6 * k + 6, :]
    def a2a(i):
        peer = (sq + i) % 16
        return pltpu.make_async_remote_copy(stage.at[peer], recv.at[sq], as_.at[i], ar_.at[i], device_id=(dp, peer), device_id_type=MESH)
    for i in range(1, 16):
        a2a(i).start()
    recv[sq] = stage[sq]
    for i in range(1, 8):
        dpx(i).wait_recv()
    gsum[...] = jnp.sum(gdp[...], axis=0)
    def inf(i):
        peer = (sq + i) % 16
        return pltpu.make_async_remote_copy(gsum, gsq.at[sq], is_.at[i], ir_.at[i], device_id=(dp, peer), device_id_type=MESH)
    for i in range(1, 16):
        inf(i).start()
    gsq[sq] = gsum[...]
    for i in range(1, 16):
        a2a(i).wait_recv()
    for s in range(16):
        oA[:, s // 2, 384 * (s % 2):384 * (s % 2) + 384] = recv[s, 0:6, 0:384]
        oB[:, s // 8, 256 * (s % 8):256 * (s % 8) + 256] = recv[s, 0:6, 384:640]
    for i in range(1, 16):
        inf(i).wait_recv()
    oG[...] = pltpu.roll(jnp.sum(gsq[...], axis=0), (128 - 6 * sq) % 128, 1)
    for i in range(1, 8):
        dpx(i).wait_send()
    for i in range(1, 16):
        a2a(i).wait_send()
        inf(i).wait_send()
    for n in range(6):
        for j in range(4):
            sib_copy(n, j).wait_send()
        for t in range(3):
            for k in kinds(n, t):
                hop_send(n, t, k).wait_send()
            fin_send(n, t, 0).wait_send()
            fin_send(n, t, 1).wait_send()

def scatter(GA, GB, GC, gg):
    V = pl.BlockSpec(memory_space=pltpu.VMEM)
    H = pl.BlockSpec(memory_space=pltpu.HBM)
    D = pltpu.SemaphoreType.DMA
    bA, bB, bC = (32, 384), (48, 256), (16, 768)
    M = lambda *s: pltpu.VMEM(s, BF)
    trip = lambda pre: [M(3, *pre, *bA), M(2, *pre, *bB), M(*pre, *bC)]
    return pl.pallas_call(
        scatter_kernel,
        out_shape=(jax.ShapeDtypeStruct((6, 8, 768), F32), jax.ShapeDtypeStruct((6, 2, 2048), F32),
                   jax.ShapeDtypeStruct((16, 768), F32), jax.ShapeDtypeStruct((8, 128), F32)),
        in_specs=[H] * 3 + [V], out_specs=(V,) * 4,
        scratch_shapes=trip((4, 4, 4)) + trip((4, 4, 4)) + trip((2, 2, 4)) + trip((2, 4, 4)) + trip((2, 2)) + trip((2, 4)) + trip((2,)) + trip((2,))
        + [pltpu.VMEM((96, 640), F32), pltpu.VMEM((16, 8, 640), F32), pltpu.VMEM((16, 8, 640), F32),
           pltpu.VMEM((8, 8, 128), F32), pltpu.VMEM((8, 128), F32), pltpu.VMEM((16, 8, 128), F32),
           D((6, 3, 4)), D((6, 3, 4)), D((6, 4)), D((6, 4)), D((6, 4)), D((16,)), D((16,)), D((16,)), D((16,)), D((8,)), D((8,))],
        compiler_params=pltpu.CompilerParams(collective_id=1, has_side_effects=True, vmem_limit_bytes=60 << 20),
        name="scatter_grads",
    )(GA, GB, GC, gg)

NEG = -1e30
PLANE = ((0, "xy"), (1, "yx"))

class Plane:
    def __init__(self, me, view, ss, rs):
        self.me, self.view, self.ss, self.rs = me, view, ss, rs
    def group(self, n, t, step, half=None):
        order = PLANE[n][1]
        at = moved(self.me, order[t], step)
        if t:
            at = {**at, order[0]: ALL if half is None else pl.ds(2 * half, 2)}
        return at
    def copy(self, n, t, kind, back=0):
        axis = PLANE[n][1][t]
        step = 1 if kind in (0, 2) else -1
        at = self.group(n, t, back) if kind < 2 else self.group(n, t, back - step, kind - 2)
        v = self.view(n, at)
        return pltpu.make_async_remote_copy(v, v, self.ss.at[n, t, kind], self.rs.at[n, t, kind], device_id=dev(moved(self.me, axis, step)), device_id_type=MESH)
    def arrived(self, n, t, kind):
        step = 1 if kind in (0, 2) else -1
        self.copy(n, t, kind, -step).wait_recv()
    def kinds(self, n, t):
        return (0, 1, 2, 3) if t else (0, 1, 2 + n)
    def send(self, t):
        for n in range(2):
            if t:
                for k in self.kinds(n, t - 1)[2:]:
                    self.arrived(n, t - 1, k)
            self.copy(n, t, 0).start()
            self.copy(n, t, 1).start()
    def forward(self, t):
        for n in range(2):
            for k in (0, 1):
                self.arrived(n, t, k)
                if 2 + k in self.kinds(n, t):
                    self.copy(n, t, 2 + k).start()
    def finish(self):
        for n in range(2):
            for k in (2, 3):
                self.arrived(n, 1, k)
    def drain(self):
        for n in range(2):
            for t in range(2):
                for k in self.kinds(n, t):
                    self.copy(n, t, k).wait_send()

def meet(dp, sq):
    bar = pltpu.get_barrier_semaphore()
    for i in range(1, 16):
        pl.semaphore_signal(bar, inc=1, device_id=(dp, (sq + i) % 16), device_id_type=MESH)
    return bar

def offset(me, j, sign=1):
    return {**me, "x": (me["x"] + sign * (j // 4) + 4) % 4, "y": (me["y"] + sign * (j % 4) + 4) % 4}

def head_masks(value=1.0):
    lane = lax.broadcasted_iota(jnp.int32, (1, 256), 1)
    return [jnp.where(lane // 64 == h, value, 0.0).astype(BF) for h in range(4)]

def dot(a, b, ca=1, cb=0):
    return lax.dot_general(a, b, (((ca,), (cb,)), ((), ())), preferred_element_type=F32)

def cross_fwd_kernel(q, lens, mem_h, A, q_h, k_h, v_h, kt_h, o_ref, L_ref,
                     qall, mem, wk, wv, wkT, wvT, K, V, KT, VT, ost, lst, orc, lrc, acc,
                     mem_s, w_s, out_s, ss, rs, os_, or_, ls_, lr_):
    me = where_am_i()
    dp, sq = lax.axis_index("dp"), lax.axis_index("seq")
    bar = meet(dp, sq)
    def load_mem(e):
        return pltpu.make_async_copy(mem_h.at[e], mem.at[e], mem_s.at[e])
    loads = [pltpu.make_async_copy(A.at[10 + i], (wk if i < 2 else wv).at[:, pl.ds(384 * (i % 2), 384)], w_s.at[i]) for i in range(4)]
    for c in loads:
        c.start()
    @pl.loop(0, 16)
    def _(e):
        load_mem(e).start()
    qall[me["x"], me["y"]] = q[...]
    pl.semaphore_wait(bar, 15)
    plane = Plane(me, lambda n, at: qall.at[at["x"], at["y"], :, pl.ds(384 * n, 384)], ss, rs)
    plane.send(0)
    for c in loads:
        c.wait()
    for i in range(6):
        wkT[:, 128 * i:128 * i + 128] = wk[128 * i:128 * i + 128, :].T
        wvT[:, 128 * i:128 * i + 128] = wv[128 * i:128 * i + 128, :].T
    plane.forward(0)
    def project(a, b):
        @pl.loop(a, b)
        def _(e):
            load_mem(e).wait()
            m = mem[e]
            K[e] = dot(m, wk[...]).astype(BF)
            VT[e] = dot(wvT[...], m, 1, 1).astype(BF)
            V[e] = dot(m, wv[...]).astype(BF)
            KT[e] = dot(wkT[...], m, 1, 1).astype(BF)
    project(0, 4)
    plane.send(1)
    project(4, 12)
    plane.forward(1)
    project(12, 16)
    outs = [pltpu.make_async_copy(a, b, out_s.at[i]) for i, (a, b) in enumerate(((K, k_h), (V, v_h), (KT, kt_h), (qall, q_h)))]
    for c in outs[:3]:
        c.start()
    plane.finish()
    outs[3].start()
    masks = head_masks()
    pos = (192 * sq + lax.broadcasted_iota(jnp.int32, (192, 128), 0)).astype(F32)
    def o_copy(j):
        return pltpu.make_async_remote_copy(ost.at[j], orc.at[j], os_.at[j], or_.at[j], device_id=dev(offset(me, j)), device_id_type=MESH)
    def l_copy(j):
        return pltpu.make_async_remote_copy(lst.at[j], lrc.at[j], ls_.at[j], lr_.at[j], device_id=dev(offset(me, j)), device_id_type=MESH)
    @pl.loop(0, 16)
    def _(i):
        j = (i + 1) % 16
        at = offset(me, j)
        e = at["x"] * 4 + at["y"]
        live = pos < lens[pl.ds(e, 1), :]
        for g in range(3):
            q4 = qall[at["x"], at["y"], :, 256 * g:256 * g + 256]
            q4s = jnp.concatenate([q4 * m for m in masks], axis=0)
            sT = dot(K[e, :, 256 * g:256 * g + 256], q4s, 1, 1)
            ps, inv = [], []
            for h in range(4):
                s = jnp.where(live, sT[:, 128 * h:128 * h + 128], NEG)
                top = jnp.max(s, axis=0, keepdims=True)
                p = jnp.exp(s - top)
                tot = jnp.sum(p, axis=0, keepdims=True)
                lst[j, 4 * g + h:4 * g + h + 1, :] = top + jnp.log(tot)
                ps.append(p.astype(BF))
                inv.append(1.0 / tot)
            oT = dot(VT[e, 256 * g:256 * g + 256, :], jnp.concatenate(ps, axis=1))
            for h in range(4):
                ost[j, 256 * g + 64 * h:256 * g + 64 * h + 64, :] = (oT[64 * h:64 * h + 64, 128 * h:128 * h + 128] * inv[h]).astype(BF)
        @pl.when(j > 0)
        def _():
            l_copy(j).start()
            o_copy(j).start()
    lrc[0] = lst[0]
    orc[0] = ost[0]
    @pl.loop(1, 16)
    def _(j):
        l_copy(j).wait_recv()
    l = lrc[:, 0:12, :]
    top = jnp.max(l, axis=0)
    total = top + jnp.log(jnp.sum(jnp.exp(l - top[None]), axis=0))
    L_ref[0:12, :] = total
    L_ref[12:16, :] = jnp.zeros((4, 128), F32)
    acc[...] = jnp.zeros_like(acc)
    @pl.loop(0, 16)
    def _(j):
        @pl.when(j > 0)
        def _():
            o_copy(j).wait_recv()
        w = jnp.exp(lrc[j, 0:12, :] - L_ref[0:12, :])
        for h in range(12):
            acc[64 * h:64 * h + 64, :] += orc[j, 64 * h:64 * h + 64, :].astype(F32) * w[h:h + 1, :]
    for i in range(6):
        o_ref[:, 128 * i:128 * i + 128] = acc[128 * i:128 * i + 128, :].T
    @pl.loop(1, 16)
    def _(j):
        l_copy(j).wait_send()
        o_copy(j).wait_send()
    plane.drain()
    for c in outs:
        c.wait()

def cross_fwd(q, lens, memory, A):
    V = pl.BlockSpec(memory_space=pltpu.VMEM)
    H = pl.BlockSpec(memory_space=pltpu.HBM)
    D = pltpu.SemaphoreType.DMA
    S = jax.ShapeDtypeStruct
    M = lambda *s: pltpu.VMEM(s, BF)
    return pl.pallas_call(
        cross_fwd_kernel,
        out_shape=(S((4, 4, 128, 768), BF), S((16, 192, 768), BF), S((16, 192, 768), BF), S((16, 768, 192), BF), S((128, 768), F32), S((16, 128), F32)),
        in_specs=[V, V, H, H], out_specs=(H, H, H, H, V, V),
        scratch_shapes=[M(4, 4, 128, 768), M(16, 192, 768), M(768, 768), M(768, 768), M(768, 768), M(768, 768),
                        M(16, 192, 768), M(16, 192, 768), M(16, 768, 192), M(16, 768, 192), M(16, 768, 128), pltpu.VMEM((16, 16, 128), F32),
                        M(16, 768, 128), pltpu.VMEM((16, 16, 128), F32), pltpu.VMEM((768, 128), F32),
                        D((16,)), D((4,)), D((4,)), D((2, 2, 4)), D((2, 2, 4)), D((16,)), D((16,)), D((16,)), D((16,))],
        compiler_params=pltpu.CompilerParams(collective_id=2, has_side_effects=True, vmem_limit_bytes=60 << 20),
        name="cross_forward",
    )(q, lens, memory, A)

def cross_bwd_kernel(do, st, lens, q_h, k_h, v_h, kt_h, mem_h, A, G_in, dq_ref, gm_h, dw_h,
                     qall, doall, stall, wk, wv, K, V, KT, mem, memT, dK, dV, gst, wst, dst, drc, acc,
                     ld_s, w_s, gm_s, dw_s, ss, rs, sss, srs, ds_, dr_):
    me = where_am_i()
    dp, sq = lax.axis_index("dp"), lax.axis_index("seq")
    bar = meet(dp, sq)
    lds = [pltpu.make_async_copy(a, b, ld_s.at[i]) for i, (a, b) in enumerate(((mem_h, mem), (q_h, qall), (k_h, K), (v_h, V), (kt_h, KT)))]
    lds += [pltpu.make_async_copy(A.at[10 + i], (wk if i < 2 else wv).at[:, pl.ds(384 * (i % 2), 384)], w_s.at[i]) for i in range(4)]
    for c in lds:
        c.start()
    doall[me["x"], me["y"]] = do[...]
    stall[0] = st[...]
    pl.semaphore_wait(bar, 15)
    plane = Plane(me, lambda n, at: doall.at[at["x"], at["y"], :, pl.ds(384 * n, 384)], ss, rs)
    plane.send(0)
    def st_copy(j):
        return pltpu.make_async_remote_copy(st, stall.at[j], sss.at[j], srs.at[j], device_id=dev(offset(me, j, -1)), device_id_type=MESH)
    @pl.loop(1, 16)
    def _(j):
        st_copy(j).start()
    lds[0].wait()
    def turn(a, b):
        @pl.loop(a, b)
        def _(e):
            memT[:, pl.ds(pl.multiple_of(256 * e, 256), 256)] = mem[pl.ds(pl.multiple_of(256 * e, 256), 256), :].T
    turn(0, 2)
    plane.forward(0)
    turn(2, 5)
    plane.send(1)
    turn(5, 9)
    plane.forward(1)
    turn(9, 12)
    for c in lds[1:]:
        c.wait()
    @pl.loop(1, 16)
    def _(j):
        st_copy(j).wait_recv()
    plane.finish()
    masks = head_masks()
    pos = (192 * sq + lax.broadcasted_iota(jnp.int32, (192, 128), 0)).astype(F32)
    def d_copy(j):
        return pltpu.make_async_remote_copy(dst.at[j], drc.at[j], ds_.at[j], dr_.at[j], device_id=dev(offset(me, j)), device_id_type=MESH)
    @pl.loop(0, 16)
    def _(i):
        j = (i + 1) % 16
        at = offset(me, j)
        e = at["x"] * 4 + at["y"]
        live = pos < lens[pl.ds(e, 1), :]
        rows = pl.ds(pl.multiple_of(192 * e, 192), 192)
        for g in range(3):
            cols = slice(256 * g, 256 * g + 256)
            q4 = qall[at["x"], at["y"], :, cols]
            d4 = doall[at["x"], at["y"], :, cols]
            q4s = jnp.concatenate([q4 * m for m in masks], axis=0)
            d4s = jnp.concatenate([d4 * m for m in masks], axis=0)
            sT = dot(K[e, :, cols], q4s, 1, 1)
            gT = dot(V[e, :, cols], d4s, 1, 1)
            ps, gs = [], []
            for h in range(4):
                n = 4 * g + h
                s = jnp.where(live, sT[:, 128 * h:128 * h + 128], NEG)
                p = jnp.exp(s - stall[j, n:n + 1, :])
                ps.append(p.astype(BF))
                gs.append((p * (gT[:, 128 * h:128 * h + 128] - stall[j, 16 + n:17 + n, :])).astype(BF))
            pT = jnp.concatenate(ps, axis=1)
            sg = jnp.concatenate(gs, axis=1)
            dV[rows, cols] = dot(pT, d4s).astype(BF)
            dK[rows, cols] = dot(sg, q4s).astype(BF)
            qT = dot(KT[e, cols, :], sg)
            for h in range(4):
                dst[j, 256 * g + 64 * h:256 * g + 64 * h + 64, :] = qT[64 * h:64 * h + 64, 128 * h:128 * h + 128].astype(BF)
        @pl.when(j > 0)
        def _():
            d_copy(j).start()
    def gm_copy(e):
        return pltpu.make_async_copy(gst.at[e % 2], gm_h.at[e], gm_s.at[e % 2])
    @pl.loop(0, 16)
    def _(e):
        @pl.when(e > 1)
        def _():
            gm_copy(e - 2).wait()
        rows = pl.ds(pl.multiple_of(192 * e, 192), 192)
        gst[e % 2] = dot(dK[rows, :], wk[...], 1, 1) + dot(dV[rows, :], wv[...], 1, 1)
        gm_copy(e).start()
    def dw_copy(n, r):
        return pltpu.make_async_copy(wst.at[n % 2], dw_h.at[10 + n, pl.ds(pl.multiple_of(128 * r, 128), 128)], dw_s.at[n % 2])
    for n in range(4):
        src = dK if n < 2 else dV
        @pl.loop(0, 6)
        def _(r):
            @pl.when(r > 0)
            def _():
                dw_copy(n, r - 1).wait()
            wst[n % 2] = dot(memT[pl.ds(pl.multiple_of(128 * r, 128), 128), :], src[:, 384 * (n % 2):384 * (n % 2) + 384]).astype(BF)
            dw_copy(n, r).start()
        dw_copy(n, 5).wait()
    acc[...] = dst[0].astype(F32)
    @pl.loop(1, 16)
    def _(j):
        d_copy(j).wait_recv()
        acc[...] += drc[j].astype(F32)
    for i in range(6):
        dq_ref[:, 128 * i:128 * i + 128] = 0.125 * acc[128 * i:128 * i + 128, :].T
    gm_copy(14).wait()
    gm_copy(15).wait()
    @pl.loop(1, 16)
    def _(j):
        st_copy(j).wait_send()
        d_copy(j).wait_send()
    plane.drain()

def cross_bwd(do, st, lens, q_h, k_h, v_h, kt_h, memory, A, GA):
    V = pl.BlockSpec(memory_space=pltpu.VMEM)
    H = pl.BlockSpec(memory_space=pltpu.HBM)
    D = pltpu.SemaphoreType.DMA
    S = jax.ShapeDtypeStruct
    M = lambda *s: pltpu.VMEM(s, BF)
    return pl.pallas_call(
        cross_bwd_kernel,
        out_shape=(S((128, 768), F32), S((16, 192, 768), F32), S((16, 768, 384), BF)),
        in_specs=[V, V, V, H, H, H, H, H, H, H], out_specs=(V, H, H), input_output_aliases={9: 2},
        scratch_shapes=[M(4, 4, 128, 768), M(4, 4, 128, 768), pltpu.VMEM((16, 32, 128), F32), M(768, 768), M(768, 768),
                        M(16, 192, 768), M(16, 192, 768), M(16, 768, 192), M(3072, 768), M(768, 3072), M(3072, 768), M(3072, 768),
                        pltpu.VMEM((2, 192, 768), F32), M(2, 128, 384), M(16, 768, 128), M(16, 768, 128), pltpu.VMEM((768, 128), F32),
                        D((5,)), D((4,)), D((2,)), D((2,)), D((2, 2, 4)), D((2, 2, 4)), D((16,)), D((16,)), D((16,)), D((16,))],
        compiler_params=pltpu.CompilerParams(collective_id=3, has_side_effects=True, vmem_limit_bytes=60 << 20),
        name="cross_backward",
    )(do, st, lens, q_h, k_h, v_h, kt_h, memory.reshape(3072, 768), A, GA)


def adam_update(master, first, second, grad, rate):
    first_new = beta_one * first + (1.0 - beta_one) * grad
    second_new = beta_two * second + (1.0 - beta_two) * grad * grad
    fix_one = 1.0 - beta_one**STEP
    fix_two = 1.0 - beta_two**STEP
    master_new = master - rate * (
        first_new / fix_one / (jnp.sqrt(second_new / fix_two) + adam_eps) + decay_rate * master
    )
    return (master_new, first_new, second_new, master_new.astype(jnp.bfloat16))


def rms(x):
    return lax.rsqrt(jnp.mean(x * x, axis=-1, keepdims=True) + eps_norm)

def rms_back(x, inv, gain, u):
    scaled = u * gain
    inner = jnp.mean(scaled * x, axis=-1, keepdims=True)
    return inv * scaled - x * inv * inv * inv * inner, jnp.sum(u * x * inv, axis=0, keepdims=True)

def flip(x):
    return jnp.concatenate([x[:, 128 * i:128 * i + 128].T for i in range(x.shape[1] // 128)], axis=0)

def unflip(x):
    return jnp.concatenate([x[128 * i:128 * i + 128, :].T for i in range(x.shape[0] // 128)], axis=1)

def apply_w(h, W, k):
    return jnp.concatenate([dot(h, W[2 * k]), dot(h, W[2 * k + 1])], axis=1)

def apply_wt(u, W, k):
    return dot(u[:, 0:384], W[2 * k], 1, 1) + dot(u[:, 384:768], W[2 * k + 1], 1, 1)

def causal_mask():
    return lax.broadcasted_iota(jnp.int32, (128, 128), 0) <= lax.broadcasted_iota(jnp.int32, (128, 128), 1)

def self_fwd_kernel(x_ref, gains, A, q2, h1, qkv, o1, x1, h2, L1, W, sem):
    loads = [pltpu.make_async_copy(A.at[i], W.at[i], sem.at[i]) for i in range(10)]
    for c in loads:
        c.start()
    x = x_ref[...].astype(F32)
    h = (x * rms(x) * gains[0:1, :]).astype(BF)
    h1[...] = h
    for k in range(3):
        loads[2 * k].wait()
        loads[2 * k + 1].wait()
        full = apply_w(h, W, k)
        qkv[k] = full.astype(BF)
    vT = flip(full).astype(BF)
    masks = head_masks(0.125)
    live = causal_mask()
    outs = []
    for g in range(3):
        cols = slice(256 * g, 256 * g + 256)
        q4 = qkv[0, :, cols]
        sT = dot(qkv[1, :, cols], jnp.concatenate([q4 * m for m in masks], axis=0), 1, 1)
        ps = []
        for n in range(4):
            s = jnp.where(live, sT[:, 128 * n:128 * n + 128], NEG)
            top = jnp.max(s, axis=0, keepdims=True)
            lse = top + jnp.log(jnp.sum(jnp.exp(s - top), axis=0, keepdims=True))
            L1[4 * g + n:4 * g + n + 1, :] = lse
            ps.append(jnp.exp(s - lse).astype(BF))
        oT = dot(vT[256 * g:256 * g + 256, :], jnp.concatenate(ps, axis=1))
        outs += [oT[64 * n:64 * n + 64, 128 * n:128 * n + 128] for n in range(4)]
    o = unflip(jnp.concatenate(outs, axis=0)).astype(BF)
    o1[...] = o
    for c in loads[6:]:
        c.wait()
    x = x + apply_w(o, W, 3)
    x1[...] = x
    h = (x * rms(x) * gains[1:2, :]).astype(BF)
    h2[...] = h
    q2[...] = apply_w(h, W, 4).astype(BF) * jnp.asarray(0.125, BF)

VS = pl.BlockSpec(memory_space=pltpu.VMEM)
HS = pl.BlockSpec(memory_space=pltpu.HBM)
SDS = jax.ShapeDtypeStruct

def self_fwd(x, gains, A):
    row = SDS((128, 768), BF)
    return pl.pallas_call(
        self_fwd_kernel,
        out_shape=(row, row, SDS((3, 128, 768), BF), row, SDS((128, 768), F32), row, SDS((16, 128), F32)),
        in_specs=[VS, VS, HS], out_specs=(VS,) * 7,
        scratch_shapes=[pltpu.VMEM((10, 768, 384), BF), pltpu.SemaphoreType.DMA((10,))],
        compiler_params=pltpu.CompilerParams(vmem_limit_bytes=60 << 20),
        name="self_forward",
    )(x, gains, A)

def ffn_kernel(x1, o2, L2, dy_ref, gains, A, B, C, out, do2, st, dx2, gg, GA, GB, GC,
               W7, WB, WC, gA, gB, gC, sw, sb, sc, tb, tc, ta):
    lA = [pltpu.make_async_copy(A.at[14 + i], W7.at[i], sw.at[i]) for i in range(2)]
    lB = [pltpu.make_async_copy(B.at[i], WB.at[i], sb.at[i]) for i in range(16)]
    lC = [pltpu.make_async_copy(C.at[i], WC.at[i], sc.at[i]) for i in range(8)]
    for c in lA:
        c.start()
    for j in range(8):
        lB[j].start()
        lB[8 + j].start()
        lC[j].start()
    o = o2[...]
    ob = o.astype(BF)
    for c in lA:
        c.wait()
    x = x1[...] + apply_w(ob, W7, 0)
    inv = rms(x)
    h = (x * inv * gains[2:3, :]).astype(BF)
    hT = flip(h.astype(F32)).astype(BF)
    df = dy_ref[...]
    y = jnp.zeros((128, 768), F32)
    dh = jnp.zeros((128, 768), F32)
    c0 = 0.7978845608028654
    sB, sC = [], []
    for j in range(8):
        lB[j].wait()
        lB[8 + j].wait()
        lC[j].wait()
        a = dot(h, WB[j])
        up = dot(h, WB[8 + j])
        t = jnp.tanh(c0 * (a + 0.044715 * a * a * a))
        half = 0.5 * (1.0 + t)
        gel = a * half
        der = half + 0.5 * a * (1.0 - t * t) * (c0 * (1.0 + 0.134145 * a * a))
        mid32 = gel * up
        mid = mid32.astype(BF)
        y += dot(mid, WC[j])
        dm = dot(df, WC[j], 1, 1)
        dga = (dm * up * der).astype(BF)
        dup = (dm * gel).astype(BF)
        dh += dot(dga, WB[j], 1, 1) + dot(dup, WB[8 + j], 1, 1)
        gB[j] = dot(hT, dga).astype(BF)
        gB[8 + j] = dot(hT, dup).astype(BF)
        gC[j] = dot(flip(mid32).astype(BF), df).astype(BF)
        sB += [pltpu.make_async_copy(gB.at[j], GB.at[j], tb.at[j]), pltpu.make_async_copy(gB.at[8 + j], GB.at[8 + j], tb.at[8 + j])]
        sC += [pltpu.make_async_copy(gC.at[j], GC.at[j], tc.at[j])]
        for c in sB[-2:] + sC[-1:]:
            c.start()
    out[...] = (x + y).astype(BF)
    dz, gain = rms_back(x, inv, gains[2:3, :], dh)
    gg[...] = gain
    d = df.astype(F32) + dz
    dx2[...] = d
    dc = d.astype(BF)
    dof = apply_wt(dc, W7, 0).astype(BF)
    do2[...] = dof
    prod = flip(dof.astype(F32) * o)
    st[...] = jnp.zeros((32, 128), F32)
    st[0:12, :] = L2[0:12, :]
    for n in range(12):
        st[16 + n:17 + n, :] = jnp.sum(prod[64 * n:64 * n + 64, :], axis=0, keepdims=True)
    oT = flip(o).astype(BF)
    sA = []
    for i in range(2):
        gA[i] = dot(oT, dc[:, 384 * i:384 * i + 384]).astype(BF)
        sA.append(pltpu.make_async_copy(gA.at[i], GA.at[14 + i], ta.at[i]))
        sA[-1].start()
    for c in sA + sB + sC:
        c.wait()

def ffn(x1, o2, L2, dy, gains, A, B, C):
    M = lambda *s: pltpu.VMEM(s, BF)
    D = pltpu.SemaphoreType.DMA
    return pl.pallas_call(
        ffn_kernel,
        out_shape=(SDS((128, 768), BF), SDS((128, 768), BF), SDS((32, 128), F32), SDS((128, 768), F32), SDS((1, 768), F32),
                   SDS((16, 768, 384), BF), SDS((16, 768, 256), BF), SDS((8, 256, 768), BF)),
        in_specs=[VS] * 5 + [HS] * 3, out_specs=(VS,) * 5 + (HS,) * 3,
        scratch_shapes=[M(2, 768, 384), M(16, 768, 256), M(8, 256, 768), M(2, 768, 384), M(16, 768, 256), M(8, 256, 768),
                        D((2,)), D((16,)), D((8,)), D((16,)), D((8,)), D((2,))],
        compiler_params=pltpu.CompilerParams(vmem_limit_bytes=60 << 20),
        name="feed_forward",
    )(x1, o2, L2, dy, gains, A, B, C)

def self_bwd_kernel(dq2, h2, x1, dx2, qkv, o1, L1, x_ref, h1, gains, g3, A, GA_in, gm_in, gin, tile, GA, gm,
                    W, G, gb, gmv, sem, gsem, msem):
    loads = [pltpu.make_async_copy(A.at[i], W.at[i], sem.at[i]) for i in range(10)]
    for i in (8, 9, 6, 7, 0, 1, 2, 3, 4, 5):
        loads[i].start()
    def gm_load(e):
        return pltpu.make_async_copy(gm_in.at[e], gmv.at[e], msem.at[e])
    def gm_store(e):
        return pltpu.make_async_copy(gmv.at[e], gm.at[e], msem.at[16 + e])
    for e in range(16):
        gm_load(e).start()
    stores = []
    def weight_grad(k, left, inc):
        for i in range(2):
            n = 2 * k + i
            G[n] = dot(left, inc[:, 384 * i:384 * i + 384]).astype(BF)
            stores.append(pltpu.make_async_copy(G.at[n], GA.at[n], gsem.at[n]))
            stores[-1].start()
    dqb = dq2[...].astype(BF)
    for i in (8, 9, 6, 7):
        loads[i].wait()
    u = apply_wt(dqb, W, 4)
    x = x1[...]
    inv = rms(x)
    dz, gain = rms_back(x, inv, gains[1:2, :], u)
    gb[...] = jnp.zeros((8, 768), F32)
    gb[1:2, :] = gain
    gb[2:3, :] = g3[...]
    d1 = dx2[...] + dz
    da = d1.astype(BF)
    do1 = apply_wt(da, W, 3).astype(BF)
    weight_grad(4, flip(h2[...].astype(F32)).astype(BF), dqb)
    masks = head_masks(0.125)
    ones = head_masks(1.0)
    live = causal_mask()
    kT = flip(qkv[1].astype(F32)).astype(BF)
    qs, ks, vs = [], [], []
    for g in range(3):
        cols = slice(256 * g, 256 * g + 256)
        q4 = qkv[0, :, cols]
        d4 = do1[:, cols]
        q4s = jnp.concatenate([q4 * m for m in masks], axis=0)
        d4s = jnp.concatenate([d4 * m for m in ones], axis=0)
        sT = dot(qkv[1, :, cols], q4s, 1, 1)
        gT = dot(qkv[2, :, cols], d4s, 1, 1)
        ps, gs = [], []
        for n in range(4):
            s = jnp.where(live, sT[:, 128 * n:128 * n + 128], NEG)
            p = jnp.exp(s - L1[4 * g + n:4 * g + n + 1, :])
            gt = gT[:, 128 * n:128 * n + 128]
            ps.append(p.astype(BF))
            gs.append((p * (gt - jnp.sum(p * gt, axis=0, keepdims=True))).astype(BF))
        sg = jnp.concatenate(gs, axis=1)
        vs.append(dot(jnp.concatenate(ps, axis=1), d4s).astype(BF))
        ks.append(dot(sg, q4s).astype(BF))
        qT = dot(kT[256 * g:256 * g + 256, :], sg)
        qs += [qT[64 * n:64 * n + 64, 128 * n:128 * n + 128] for n in range(4)]
    for e in range(16):
        gm_load(e).wait()
        gm_store(e).start()
    inc = [(0.125 * unflip(jnp.concatenate(qs, axis=0))).astype(BF), jnp.concatenate(ks, axis=1), jnp.concatenate(vs, axis=1)]
    weight_grad(3, flip(o1[...].astype(F32)).astype(BF), da)
    for c in loads[:6]:
        c.wait()
    u = apply_wt(inc[0], W, 0) + apply_wt(inc[1], W, 1) + apply_wt(inc[2], W, 2)
    x = x_ref[...].astype(F32)
    inv = rms(x)
    dz, gain = rms_back(x, inv, gains[0:1, :], u)
    gb[0:1, :] = gain
    gin[...] = d1 + dz
    hT = flip(h1[...].astype(F32)).astype(BF)
    for k in range(3):
        weight_grad(k, hT, inc[k])
    lane = lax.broadcasted_iota(jnp.int32, (8, 128), 1)
    for d in range(8):
        lo, sh = 96 * d // 128, 96 * d % 128
        t = pltpu.roll(gb[:, 128 * lo:128 * lo + 128], (128 - sh) % 128, 1)
        if sh > 32:
            nxt = pltpu.roll(gb[:, 128 * lo + 128:128 * lo + 256], (128 - sh) % 128, 1)
            t = jnp.where(lane < 128 - sh, t, nxt)
        tile[d] = jnp.where(lane < 96, t, 0.0)
    for c in stores:
        c.wait()
    for e in range(16):
        gm_store(e).wait()

def self_bwd(dq2, h2, x1, dx2, qkv, o1, L1, x, h1, gains, g3, A, GA, gm):
    D = pltpu.SemaphoreType.DMA
    return pl.pallas_call(
        self_bwd_kernel,
        out_shape=(SDS((128, 768), F32), SDS((8, 8, 128), F32), SDS((16, 768, 384), BF), SDS((16, 192, 768), F32)),
        in_specs=[VS] * 11 + [HS] * 3, out_specs=(VS, VS, HS, HS),
        input_output_aliases={12: 2},
        scratch_shapes=[pltpu.VMEM((10, 768, 384), BF), pltpu.VMEM((10, 768, 384), BF), pltpu.VMEM((8, 768), F32), pltpu.VMEM((16, 192, 768), F32), D((10,)), D((10,)), D((32,))],
        compiler_params=pltpu.CompilerParams(vmem_limit_bytes=60 << 20),
        name="self_backward",
    )(dq2, h2, x1, dx2, qkv, o1, L1, x, h1, gains, g3, A, GA, gm)

def adam_kernel(*refs):
    ins, outs = refs[:16], refs[16:]
    for n in range(4):
        w, m, v, g = ins[4 * n:4 * n + 4]
        grad = g[0:3, 0:6] if n == 3 else g[...]
        for o, val in zip(outs[4 * n:4 * n + 4], adam_update(w[...], m[...], v[...], grad, rate_gain if n == 3 else rate_matrix)):
            o[...] = val

def adam(*args):
    shapes = []
    for n in range(4):
        s = args[4 * n].shape
        shapes += [SDS(s, F32)] * 3 + [SDS(s, BF)]
    return pl.pallas_call(adam_kernel, out_shape=tuple(shapes), in_specs=[VS] * 16, out_specs=(VS,) * 16,
                          compiler_params=pltpu.CompilerParams(vmem_limit_bytes=60 << 20), name="adam")(*args)


def body(
    dec_input,
    memory,
    mem_len,
    grad_out,
    attn_master,
    ffn_in_master,
    ffn_out_master,
    gain_master,
    attn_first,
    ffn_in_first,
    ffn_out_first,
    gain_first,
    attn_second,
    ffn_in_second,
    ffn_out_second,
    gain_second,
):
    swap = lambda a: a.transpose(1, 0, 2)
    attn_t, in_t = swap(attn_master), swap(ffn_in_master)
    gath_a, gath_b, gath_c, gains, lens = gather(attn_t, in_t, ffn_out_master, info_tile(gain_master, mem_len))
    aw = gath_a.reshape(16, 768, 384)
    x = dec_input[0]
    q2, h1, qkv, o1, x1, h2, L1 = self_fwd(x, gains, aw)
    q_all, k_two, v_two, kt_two, o2, L2 = cross_fwd(q2, lens, memory, aw)
    out_block, do2, st, dx2, g3, GA, GB, GC = ffn(x1, o2, L2, grad_out[0], gains, aw, gath_b.reshape(16, 768, 256), gath_c.reshape(8, 256, 768))
    dq2, gm, GA = cross_bwd(do2, st, lens, q_all, k_two, v_two, kt_two, memory, aw, GA)
    grad_input, tile_g, GA, grad_memory = self_bwd(dq2, h2, x1, dx2, qkv, o1, L1, x, h1, gains, g3, aw, GA, gm)
    share_a, share_b, share_c, share_g = scatter(
        GA.reshape(4, 4, 4, 2, 3, 32, 384), GB.reshape(4, 4, 4, 2, 2, 48, 256), GC.reshape(4, 2, 4, 4, 16, 768), tile_g
    )
    new = adam(
        attn_t, swap(attn_first), swap(attn_second), share_a,
        in_t, swap(ffn_in_first), swap(ffn_in_second), share_b,
        ffn_out_master, ffn_out_first, ffn_out_second, share_c,
        gain_master, gain_first, gain_second, share_g,
    )
    return (out_block[None], grad_input[None], grad_memory, *[swap(a) for a in new[:8]], *new[8:])


def solution(mesh):
    placed = (
        P(("dp", "seq"), None, None),
        P("dp", "seq", None),
        P(("dp", "seq")),
        P(("dp", "seq"), None, None),
        P(None, ("dp", "seq"), None),
        P(None, ("dp", "seq"), None),
        P(("dp", "seq"), None),
        P(None, ("dp", "seq")),
        P(None, ("dp", "seq"), None),
        P(None, ("dp", "seq"), None),
        P(("dp", "seq"), None),
        P(None, ("dp", "seq")),
        P(None, ("dp", "seq"), None),
        P(None, ("dp", "seq"), None),
        P(("dp", "seq"), None),
        P(None, ("dp", "seq")),
    )
    return jax.shard_map(
        body,
        mesh=mesh,
        in_specs=placed,
        out_specs=(
            P(("dp", "seq"), None, None),
            P(("dp", "seq"), None, None),
            P("dp", "seq", None),
            P(None, ("dp", "seq"), None),
            P(None, ("dp", "seq"), None),
            P(None, ("dp", "seq"), None),
            P(None, ("dp", "seq"), None),
            P(None, ("dp", "seq"), None),
            P(None, ("dp", "seq"), None),
            P(None, ("dp", "seq"), None),
            P(None, ("dp", "seq"), None),
            P(("dp", "seq"), None),
            P(("dp", "seq"), None),
            P(("dp", "seq"), None),
            P(("dp", "seq"), None),
            P(None, ("dp", "seq")),
            P(None, ("dp", "seq")),
            P(None, ("dp", "seq")),
            P(None, ("dp", "seq")),
        ),
        check_vma=False,
    )
```

profile of v0, /device:TPU:0, one launch (start us, length us, event | category | flops | bytes accessed | tf_op | source)
XLA Modules:
  0.0 354.7 jit_solution(15324903019732929236)
XLA Ops:
  1.3 0.7 convert_convert_fusion
  2.0 0.2 dynamic_update_slice.6
  2.2 0.1 dynamic_update_slice.7.info
  2.3 0.0 copy-start
  2.3 0.6 copy-done
  2.9 63.5 %gather_weights.1 = (bf16[4,4,4,2,3,32,384]{6,5,4,3,2,1,0:T(8,128)(2,1)}, bf16[4,4,4,2,2,48,256]{6,5,4,3,2,1,0:T(8,128)(2,1)}, bf16[4,2,4,4,16,768]{5,4,3,2,1,0:...) custom-call(f32[6,8,768]{2,1,0:T(8,128)} %bitcast.39, f32[6,2,2048]{2,1,0:T(2,128)} %bitcast.41, f32[16,768]{1,0:T(8,128)} %refs_8_.1, ...), custom_call_target="tpu_custom_call" | custom-call | tf_op jit(solution)/shard_map/gather_weights/pallas_call | solution.py:185
  66.4 5.9 %self_forward.1 = (bf16[128,768]{1,0:T(8,128)(2,1)}, bf16[128,768]{1,0:T(8,128)(2,1)}, bf16[3,128,768]{2,1,0:T(8,128)(2,1)}, bf16[128,768]{1,0:T(8,128)(2,1)}, f...) custom-call(bf16[128,768]{1,0:T(8,128)(2,1)} %bitcast.37, f32[8,768]{1,0:T(8,128)} %get-tuple-element.72.gains, ...), custom_call_target="tpu_custom_call" | custom-call | tf_op jit(solution)/shard_map/self_forward/pallas_call | solution.py:838
  72.3 85.7 %cross_forward.1 = (bf16[4,4,128,768]{3,2,1,0:T(8,128)(2,1)}, bf16[16,192,768]{2,1,0:T(8,128)(2,1)}, bf16[16,192,768]{2,1,0:T(8,128)(2,1)}, bf16[16,768,192]{2,1...) custom-call(bf16[128,768]{1,0:T(8,128)(2,1)} %get-tuple-element.75.q, f32[16,128]{1,0:T(8,128)} %get-tuple-element.76.lens, ...), custom_call_target="tpu_custom_call" | custom-call | tf_op jit(solution)/shard_map/cross_forward/pallas_call | solution.py:617
  158.0 19.4 %feed_forward.1 = (bf16[128,768]{1,0:T(8,128)(2,1)}, bf16[128,768]{1,0:T(8,128)(2,1)}, f32[32,128]{1,0:T(8,128)}, f32[128,768]{1,0:T(8,128)}, f32[1,768]{1,0:T(1...) custom-call(f32[128,768]{1,0:T(8,128)} %get-tuple-element.74.x1, ...), custom_call_target="tpu_custom_call" | custom-call | tf_op jit(solution)/shard_map/feed_forward/pallas_call | solution.py:920
  177.4 96.7 %cross_backward.1 = (f32[128,768]{1,0:T(8,128)}, f32[16,192,768]{2,1,0:T(8,128)}, bf16[16,768,384]{2,1,0:T(8,128)(2,1)}) custom-call(bf16[128,768]{1,0:T(8,128)(2,1)} %get-tuple-element.82.do, f32[32,128]{1,0:T(8,128)} %get-tuple-element.83.st, f32[16,128]{1,0:T(8,128)} %get-tuple-element.76.lens, ...), custom_call_target="tpu_custom_call", output_to_operand_aliasing={{2}: (9, {})} | custom-call | tf_op jit(solution)/shard_map/cross_backward/pallas_call | solution.py:746
  274.0 13.7 %self_backward.1 = (f32[128,768]{1,0:T(8,128)}, f32[8,8,128]{2,1,0:T(8,128)}, bf16[16,768,384]{2,1,0:T(8,128)(2,1)}, f32[16,192,768]{2,1,0:T(8,128)}) custom-call(f32[128,768]{1,0:T(8,128)} %get-tuple-element.89.dq2, bf16[128,768]{1,0:T(8,128)(2,1)} %get-tuple-element.90.h2, f32[128,768]{1,0:T(8,128)} %get-tuple-element.74.x1, ...), custom_call_target="tpu_custom_call", output_to_operand_aliasing={{2}: (12, {})} | custom-call | tf_op jit(solution)/shard_map/self_backward/pallas_call | solution.py:1019
  287.8 64.3 %scatter_grads.1 = (f32[6,8,768]{2,1,0:T(8,128)}, f32[6,2,2048]{2,1,0:T(2,128)}, f32[16,768]{1,0:T(8,128)}, f32[8,128]{1,0:T(8,128)}) custom-call(bf16[4,4,4,2,3,32,384]{6,5,4,3,2,1,0:T(8,128)(2,1)} %bitcast.31, bf16[4,4,4,2,2,48,256]{6,5,4,3,2,1,0:T(8,128)(2,1)} %bitcast.33, bf16[4,2,4,4,16,768]{5,4,3,2,1,0:T(8,128)(2,1)} %bitcast.35, ...), custom_call_target="tpu_custom_call" | custom-call | tf_op jit(solution)/shard_map/scatter_grads/pallas_call | solution.py:432
  352.1 2.5 adam.1
  (1 shorter events, 0.0 us)
Async XLA Ops:
  2.3 0.6 copy-start
where the time goes:
time: 355 us
  Pallas kernels  352 us (99%)
    pallas_call x1, Pallas kernels, cross_bwd(): pl.pallas_call(cross_bwd_kernel, out_shape=(S((128, 768), F32), S((16, 19...  96.7 us
    pallas_call x1, Pallas kernels, cross_fwd(): pl.pallas_call(cross_fwd_kernel, out_shape=(S((4, 4, 128, 768), BF), S((1...  85.7 us
    pallas_call x1, Pallas kernels, scatter(): pl.pallas_call(scatter_kernel, out_shape=(jax.ShapeDtypeStruct((6, 8, 768...  64.3 us
    pallas_call x1, Pallas kernels, gather(): pl.pallas_call(gather_kernel, out_shape=(jax.ShapeDtypeStruct((4, 4, 4, 2...  63.5 us
    pallas_call x1, Pallas kernels, ffn(): pl.pallas_call(ffn_kernel, out_shape=(SDS((128, 768), BF), SDS((128, 768)...  19.4 us
    pallas_call x1, Pallas kernels, self_bwd(): pl.pallas_call(self_bwd_kernel, out_shape=(SDS((128, 768), F32), SDS((8,...  13.7 us

commit v1 on v0

v1 whole, which is shorter than its diff:
```python
import jax
import jax.numpy as jnp
from jax import lax
from jax.experimental import pallas as pl
from jax.experimental.pallas import tpu as pltpu
from jax.sharding import PartitionSpec as P

eps_norm = 1e-06
beta_one = 0.9
beta_two = 0.999
adam_eps = 1e-08
decay_rate = 0.01
rate_matrix = 0.12
rate_gain = 3.0
STEP = 10
MESH = pl.DeviceIdType.MESH
BF, F32 = jnp.bfloat16, jnp.float32
ALL = slice(None)
NEG = -1e30
PARTS_A = (("A", 0, "xyz"), ("A", 1, "yzx"), ("A", 2, "zxy"))
PARTS_F = (("B", 0, "xyz"), ("B", 1, "yxz"), ("C", 0, "xyz"))
PARTS_D = (("D", 0, "xy"), ("D", 1, "yx"))
AXES = {"A": "xyz", "B": "xyz", "C": "zxy", "D": "xy"}
STEPS = (2, -1, 1, 0)
VS = pl.BlockSpec(memory_space=pltpu.VMEM)
HS = pl.BlockSpec(memory_space=pltpu.HBM)
SDS = jax.ShapeDtypeStruct
DMA = pltpu.SemaphoreType.DMA


def vm(*shape):
    return pltpu.VMEM(shape, BF)


def vf(*shape):
    return pltpu.VMEM(shape, F32)


def where_am_i():
    dp, sq = lax.axis_index("dp"), lax.axis_index("seq")
    return {"x": sq // 4, "y": sq % 4, "z": dp // 2, "c": dp % 2}


def dev(at):
    return (at["z"] * 2 + at["c"], at["x"] * 4 + at["y"])


def moved(at, axis, step):
    return {**at, axis: (at[axis] + step + 4) % 4}


def offset(me, j, sign=1):
    return {**me, "x": (me["x"] + sign * (j // 4) + 4) % 4, "y": (me["y"] + sign * (j % 4) + 4) % 4}


def sibling_of(me):
    return {**me, "c": 1 - me["c"]}


def remote(src, dst, send, recv, to):
    return pltpu.make_async_remote_copy(src, dst, send, recv, device_id=dev(to), device_id_type=MESH)


def meet(me, column):
    dp, sq = lax.axis_index("dp"), lax.axis_index("seq")
    bar = pltpu.get_barrier_semaphore()
    for i in range(1, 16):
        pl.semaphore_signal(bar, inc=1, device_id=(dp, (sq + i) % 16), device_id_type=MESH)
    if column == "dp":
        for i in range(1, 8):
            pl.semaphore_signal(bar, inc=1, device_id=((dp + i) % 8, sq), device_id_type=MESH)
        return bar, 22
    if column == "z":
        for to in (moved(me, "z", 1), moved(me, "z", -1), sibling_of(me)):
            pl.semaphore_signal(bar, inc=1, device_id=dev(to), device_id_type=MESH)
        return bar, 18
    return bar, 15


def dot(a, b, ca=1, cb=0):
    return lax.dot_general(a, b, (((ca,), (cb,)), ((), ())), preferred_element_type=F32)


class Gather:
    def __init__(self, me, orders, view, own, ss, rs, sib_s=None, sib_r=None):
        self.me, self.orders, self.view, self.own = me, orders, view, own
        self.ss, self.rs, self.sib_s, self.sib_r = ss, rs, sib_s, sib_r
        self.count, self.last = len(orders), len(orders[0]) - 1

    def group(self, n, t, step, half=None):
        order = self.orders[n]
        at = moved(self.me, order[t], step)
        for j in range(t):
            at = {**at, order[j]: ALL}
        if half is not None and t:
            at = {**at, order[0]: pl.ds(2 * half, 2)}
        return at

    def kinds(self, n, t):
        return (0, 1, 2, 3) if t else (0, 1, 2 + n % 2)

    def copy(self, n, t, kind, back=0):
        axis = self.orders[n][t]
        step = 1 if kind in (0, 2) else -1
        dst = self.view(n, self.group(n, t, back) if kind < 2 else self.group(n, t, back - step, kind - 2))
        src = self.own(n) if t == 0 and kind < 2 and back == 0 else dst
        return remote(src, dst, self.ss.at[n, t, kind], self.rs.at[n, t, kind], moved(self.me, axis, step))

    def arrived(self, n, t, kind):
        self.copy(n, t, kind, -1 if kind in (0, 2) else 1).wait_recv()

    def sibling(self, n, j, c):
        v = self.view(n, {**self.group(n, self.last, (0, -1, 1, 2)[j]), "c": c})
        return remote(v, v, self.sib_s.at[n, j], self.sib_r.at[n, j], sibling_of(self.me))

    def send(self, t):
        for n in range(self.count):
            if t:
                for k in self.kinds(n, t - 1)[2:]:
                    self.arrived(n, t - 1, k)
            self.copy(n, t, 0).start()
            self.copy(n, t, 1).start()
            if self.sib_s is not None and t == self.last:
                self.sibling(n, 0, self.me["c"]).start()

    def forward(self, t):
        for n in range(self.count):
            for k in (0, 1):
                self.arrived(n, t, k)
                if 2 + k in self.kinds(n, t):
                    self.copy(n, t, 2 + k).start()
                if self.sib_s is not None and t == self.last:
                    self.sibling(n, 1 + k, self.me["c"]).start()

    def finish(self):
        for n in range(self.count):
            for k in (2, 3):
                self.arrived(n, self.last, k)
            if self.sib_s is not None:
                self.sibling(n, 3, self.me["c"]).start()

    def siblings_in(self):
        for n in range(self.count):
            for j in range(4):
                self.sibling(n, j, 1 - self.me["c"]).wait_recv()

    def drain(self):
        for n in range(self.count):
            for t in range(self.last + 1):
                for k in self.kinds(n, t):
                    self.copy(n, t, k).wait_send()
            if self.sib_s is not None:
                for j in range(4):
                    self.sibling(n, j, self.me["c"]).wait_send()


class Scatter:
    def __init__(self, me, parts, acc, hop, fin, ss, rs, sib=None, source=None, sib_s=None, sib_r=None, loc_s=None):
        self.me, self.parts, self.acc, self.hop_b, self.fin_b = me, parts, acc, hop, fin
        self.ss, self.rs, self.sib, self.source = ss, rs, sib, source
        self.sib_s, self.sib_r, self.loc_s = sib_s, sib_r, loc_s
        self.count, self.last = len(parts), len(parts[0][2]) - 1

    def idx(self, n, at):
        name, p, _ = self.parts[n]
        place = tuple(at[a] for a in AXES[name])
        return place if name == "C" else (p,) + place

    def slot(self, n):
        name, p, _ = self.parts[n]
        return () if name == "C" else (p,)

    def done(self, n, t):
        name, _, order = self.parts[n]
        return [a for a in AXES[name] if a in order[:t]]

    def group(self, n, t, step, half=None):
        order = self.parts[n][2]
        at = moved(self.me, order[t], step)
        for j in range(t):
            at = {**at, order[j]: ALL}
        if half is not None and t:
            at = {**at, self.done(n, t)[0]: pl.ds(2 * half, 2)}
        return at

    def kinds(self, n, t):
        return (0, 1) if t else (n % 2,)

    def refs(self, n, t):
        name = self.parts[n][0]
        return self.acc[name], self.hop_b[t][name], self.fin_b[t][name]

    def hop_copy(self, n, t, kind):
        step = 1 if kind == 0 else -1
        a, h, _ = self.refs(n, t)
        return remote(a.at[self.idx(n, self.group(n, t, 2 * step, kind))], h.at[self.slot(n) + (kind,)],
                      self.ss.at[n, t, kind], self.rs.at[n, t, kind], moved(self.me, self.parts[n][2][t], step))

    def fin_copy(self, n, t, kind):
        step = 1 if kind == 0 else -1
        a, _, f = self.refs(n, t)
        return remote(a.at[self.idx(n, self.group(n, t, step))], f.at[self.slot(n) + (kind,)],
                      self.ss.at[n, t, 2 + kind], self.rs.at[n, t, 2 + kind], moved(self.me, self.parts[n][2][t], step))

    def each(self, n, t, at, fn, half=None):
        axes = self.done(n, t)
        sizes, offs = [4] * len(axes), [0] * len(axes)
        if half is not None and axes:
            sizes[0], offs[0] = 2, 2 * half
        total = 1
        for s in sizes:
            total *= s

        def one(i):
            pos, rest = [], i
            for s in sizes[::-1]:
                pos.append(rest % s)
                rest = rest // s
            pos = pos[::-1]
            where = dict(at)
            for a, p, o in zip(axes, pos, offs):
                where[a] = p + o
            fn(self.idx(n, where), tuple(pos))

        if total == 1:
            one(0)
        else:
            pl.loop(0, total)(one)

    def sib_copy(self, n, j):
        at = self.group(n, self.last, STEPS[j])
        return remote(self.source(n, at, 1 - self.me["c"]), self.sib[self.parts[n][0]].at[self.idx(n, at)],
                      self.sib_s.at[n, j], self.sib_r.at[n, j], sibling_of(self.me))

    def loc_copy(self, n, j):
        at = self.group(n, self.last, STEPS[j])
        return pltpu.make_async_copy(self.source(n, at, self.me["c"]), self.acc[self.parts[n][0]].at[self.idx(n, at)], self.loc_s.at[n, j])

    def start(self):
        for j in range(4):
            for n in range(self.count):
                self.sib_copy(n, j).start()
                self.loc_copy(n, j).start()

    def merge(self, j):
        for n in range(self.count):
            self.sib_copy(n, j).wait_recv()
            self.loc_copy(n, j).wait()
            a, b = self.acc[self.parts[n][0]], self.sib[self.parts[n][0]]

            def fn(i, _):
                a[i] = (a[i].astype(F32) + b[i].astype(F32)).astype(BF)

            self.each(n, self.last, self.group(n, self.last, STEPS[j]), fn)

    def hop(self, t):
        for n in range(self.count):
            for k in self.kinds(n, t):
                self.hop_copy(n, t, k).start()

    def pass_on(self, t):
        for n in range(self.count):
            a, h, _ = self.refs(n, t)
            for k in (0, 1):
                if k in self.kinds(n, t):
                    self.hop_copy(n, t, k).wait_recv()

                    def fn(i, pos):
                        j = self.slot(n) + (k,) + pos
                        a[i] = (a[i].astype(F32) + h[j].astype(F32)).astype(BF)

                    self.each(n, t, self.group(n, t, 1 if k == 0 else -1), fn, k)
                self.fin_copy(n, t, k).start()

    def close(self, t):
        for n in range(self.count):
            self.fin_copy(n, t, 0).wait_recv()
            self.fin_copy(n, t, 1).wait_recv()
            a, _, f = self.refs(n, t)

            def fn(i, pos):
                s = self.slot(n)
                a[i] = (a[i].astype(F32) + f[s + (0,) + pos].astype(F32) + f[s + (1,) + pos].astype(F32)).astype(BF)

            self.each(n, t, self.group(n, t, 0), fn)

    def result(self, n):
        self.fin_copy(n, 0, 0).wait_recv()
        self.fin_copy(n, 0, 1).wait_recv()
        a, _, f = self.refs(n, 0)
        s = self.slot(n)
        return a[self.idx(n, self.me)].astype(F32) + f[s + (0,)].astype(F32) + f[s + (1,)].astype(F32)

    def drain(self):
        for n in range(self.count):
            if self.sib is not None:
                for j in range(4):
                    self.sib_copy(n, j).wait_send()
            for t in range(self.last + 1):
                for k in self.kinds(n, t):
                    self.hop_copy(n, t, k).wait_send()
                self.fin_copy(n, t, 0).wait_send()
                self.fin_copy(n, t, 1).wait_send()


def places(names, refs):
    return dict(zip(names, refs))


def stage_buffers(*shapes):
    out = []
    for lead in ((2, 2, 4), (2, 4, 4), (2, 2), (2, 4), (2,), (2,)):
        out += [vm(*pre, *lead, *block) for pre, block in shapes]
    return out


def staged(names, refs):
    k = len(names)
    got = [places(names, refs[k * i:k * i + k]) for i in range(6)]
    return {2: got[0], 1: got[2], 0: got[4]}, {2: got[1], 1: got[3], 0: got[5]}


def gather_kernel(attn, wi, wo, info, A, gains, lens, outB, outC, infos, stage, recv, blk, blkA, irecv,
                  ss, rs, sib_s, sib_r, as_, ar_, is_, ir_, ds_, dr_, own_s):
    me = where_am_i()
    dp, sq = lax.axis_index("dp"), lax.axis_index("seq")
    bar, count = meet(me, "dp")
    stage[:, 6:8, :] = jnp.zeros((16, 2, 640), F32)
    for s in range(16):
        stage[s, 0:6, 0:384] = attn[:, s // 2, 384 * (s % 2):384 * (s % 2) + 384]
        stage[s, 0:6, 384:640] = wi[:, s // 8, 256 * (s % 8):256 * (s % 8) + 256]
    pl.semaphore_wait(bar, count)

    def a2a(i):
        peer = (sq + i) % 16
        return pltpu.make_async_remote_copy(stage.at[peer], recv.at[sq], as_.at[i], ar_.at[i], device_id=(dp, peer), device_id_type=MESH)

    def inf(i):
        peer = (sq + i) % 16
        return pltpu.make_async_remote_copy(info, irecv.at[sq], is_.at[i], ir_.at[i], device_id=(dp, peer), device_id_type=MESH)

    for i in range(1, 16):
        a2a(i).start()
    for i in range(1, 16):
        inf(i).start()
    recv[sq] = stage[sq]
    irecv[sq] = info[...]
    outC[...] = wo[...].astype(BF)
    for i in range(1, 16):
        a2a(i).wait_recv()
    for k in range(16):
        blk[6 * k:6 * k + 6, :] = recv[k, 0:6, :]
    for p in range(3):
        blkA[p] = blk[32 * p:32 * p + 32, 0:384].astype(BF)
    for p in range(2):
        outB[p] = blk[48 * p:48 * p + 48, 384:640].astype(BF)
    place = lambda n, at: A.at[at["x"], at["y"], at["z"], at["c"], PARTS_A[n][1]]
    ring = Gather(me, [p[2] for p in PARTS_A], place, lambda n: blkA.at[n], ss, rs, sib_s, sib_r)
    owns = [pltpu.make_async_copy(blkA.at[n], place(n, me), own_s.at[n]) for n in range(3)]
    for o in owns:
        o.start()
    ring.send(0)
    ring.forward(0)
    for o in owns:
        o.wait()
    ring.send(1)
    ring.forward(1)
    ring.send(2)
    for i in range(1, 16):
        inf(i).wait_recv()
    tile = jnp.sum(irecv[...], axis=0)
    infos[dp] = tile

    def dpx(i, back=0):
        v = infos.at[(dp - back + 8) % 8]
        return pltpu.make_async_remote_copy(v, v, ds_.at[i], dr_.at[i], device_id=((dp + i) % 8, sq), device_id_type=MESH)

    for i in range(1, 8):
        dpx(i).start()
    ring.forward(2)
    for i in range(1, 8):
        dpx(i, i).wait_recv()
    lane = lax.broadcasted_iota(jnp.int32, (8, 128), 1)
    gains[...] = jnp.zeros((8, 768), F32)
    for d in range(8):
        lo, sh = 96 * d // 128, 96 * d % 128
        t = pltpu.roll(jnp.where(lane < 96, infos[d], 0.0), sh, 1)
        gains[:, 128 * lo:128 * lo + 128] += jnp.where(lane >= sh, t, 0.0)
        if sh > 32:
            gains[:, 128 * lo + 128:128 * lo + 256] += jnp.where(lane < sh, t, 0.0)
    pick = lax.broadcasted_iota(jnp.int32, (16, 128), 0) == lax.broadcasted_iota(jnp.int32, (16, 128), 1)
    lens[...] = jnp.broadcast_to(jnp.sum(jnp.where(pick, tile[3:4, :], 0.0), axis=1, keepdims=True), (16, 128))
    ring.finish()
    ring.siblings_in()
    for i in range(1, 16):
        a2a(i).wait_send()
        inf(i).wait_send()
    for i in range(1, 8):
        dpx(i).wait_send()
    ring.drain()


def gather(attn, wi, wo, info):
    return pl.pallas_call(
        gather_kernel,
        out_shape=(SDS((4, 4, 4, 2, 3, 32, 384), BF), SDS((8, 768), F32), SDS((16, 128), F32), SDS((2, 48, 256), BF), SDS((16, 768), BF)),
        in_specs=[VS] * 4, out_specs=(HS,) + (VS,) * 4,
        scratch_shapes=[vf(8, 8, 128), vf(16, 8, 640), vf(16, 8, 640), vf(96, 640), vm(3, 32, 384), vf(16, 8, 128),
                        DMA((3, 3, 4)), DMA((3, 3, 4)), DMA((3, 4)), DMA((3, 4)), DMA((16,)), DMA((16,)), DMA((16,)), DMA((16,)), DMA((8,)), DMA((8,)), DMA((3,))],
        compiler_params=pltpu.CompilerParams(collective_id=0, has_side_effects=True, vmem_limit_bytes=60 << 20),
        name="gather_attention_weights",
    )(attn, wi, wo, info)


def info_tile(gain, mem_len):
    sq = lax.axis_index("seq")
    t = jnp.zeros((8, 128), F32)
    t = lax.dynamic_update_slice(t, gain.astype(BF).astype(F32), (0, 6 * sq))
    return lax.dynamic_update_slice(t, mem_len.astype(F32)[:, None], (3, sq))


def scatter_kernel(GA, blkF, gg, oA, oB, oG, accA, sibA, h2, f2, h1, f1, h0, f0, blk, stage, recv, gdp, gsum, gsq,
                   ss, rs, sib_s, sib_r, loc_s, as_, ar_, is_, ir_, ds_, dr_):
    me = where_am_i()
    dp, sq = lax.axis_index("dp"), lax.axis_index("seq")
    bar, count = meet(me, "dp")
    pl.semaphore_wait(bar, count)
    hop, fin = staged("A", (h2, f2, h1, f1, h0, f0))
    ring = Scatter(me, PARTS_A, {"A": accA}, hop, fin, ss, rs, {"A": sibA},
                   lambda n, at, c: GA.at[at["x"], at["y"], at["z"], c, n], sib_s, sib_r, loc_s)
    ring.start()

    def dpx(i):
        peer = (dp + i) % 8
        return pltpu.make_async_remote_copy(gg.at[peer], gdp.at[dp], ds_.at[i], dr_.at[i], device_id=(peer, sq), device_id_type=MESH)

    for i in range(1, 8):
        dpx(i).start()
    gdp[dp] = gg[dp]
    ring.merge(0)
    ring.hop(2)
    ring.merge(1)
    ring.merge(2)
    ring.pass_on(2)
    ring.merge(3)
    for i in range(1, 8):
        dpx(i).wait_recv()
    gsum[...] = jnp.sum(gdp[...], axis=0)

    def inf(i):
        peer = (sq + i) % 16
        return pltpu.make_async_remote_copy(gsum, gsq.at[sq], is_.at[i], ir_.at[i], device_id=(dp, peer), device_id_type=MESH)

    for i in range(1, 16):
        inf(i).start()
    gsq[sq] = gsum[...]
    blk[:, 384:640] = blkF[...]
    stage[:, 6:8, :] = jnp.zeros((16, 2, 640), F32)
    ring.close(2)
    ring.hop(1)
    ring.pass_on(1)
    ring.close(1)
    ring.hop(0)
    ring.pass_on(0)
    for n in range(3):
        blk[32 * n:32 * n + 32, 0:384] = ring.result(n)
    for k in range(16):
        stage[k, 0:6, :] = blk[6 * k:6 * k + 6, :]

    def a2a(i):
        peer = (sq + i) % 16
        return pltpu.make_async_remote_copy(stage.at[peer], recv.at[sq], as_.at[i], ar_.at[i], device_id=(dp, peer), device_id_type=MESH)

    for i in range(1, 16):
        a2a(i).start()
    recv[sq] = stage[sq]
    for i in range(1, 16):
        inf(i).wait_recv()
    oG[...] = pltpu.roll(jnp.sum(gsq[...], axis=0), (128 - 6 * sq) % 128, 1)
    for i in range(1, 16):
        a2a(i).wait_recv()
    for s in range(16):
        oA[:, s // 2, 384 * (s % 2):384 * (s % 2) + 384] = recv[s, 0:6, 0:384]
        oB[:, s // 8, 256 * (s % 8):256 * (s % 8) + 256] = recv[s, 0:6, 384:640]
    for i in range(1, 8):
        dpx(i).wait_send()
    for i in range(1, 16):
        a2a(i).wait_send()
        inf(i).wait_send()
    ring.drain()


def scatter(GA, blkF, gg):
    return pl.pallas_call(
        scatter_kernel,
        out_shape=(SDS((6, 8, 768), F32), SDS((6, 2, 2048), F32), SDS((8, 128), F32)),
        in_specs=[HS, VS, VS], out_specs=(VS,) * 3,
        scratch_shapes=[vm(3, 4, 4, 4, 32, 384), vm(3, 4, 4, 4, 32, 384), *stage_buffers(((3,), (32, 384))),
                        vf(96, 640), vf(16, 8, 640), vf(16, 8, 640), vf(8, 8, 128), vf(8, 128), vf(16, 8, 128),
                        DMA((3, 3, 4)), DMA((3, 3, 4)), DMA((3, 4)), DMA((3, 4)), DMA((3, 4)),
                        DMA((16,)), DMA((16,)), DMA((16,)), DMA((16,)), DMA((8,)), DMA((8,))],
        compiler_params=pltpu.CompilerParams(collective_id=1, has_side_effects=True, vmem_limit_bytes=60 << 20),
        name="scatter_attention_grads",
    )(GA, blkF, gg)


def head_masks(value=1.0):
    lane = lax.broadcasted_iota(jnp.int32, (1, 256), 1)
    return [jnp.where(lane // 64 == h, value, 0.0).astype(BF) for h in range(4)]


def stack_heads(block, masks):
    return jnp.concatenate([block * m for m in masks], axis=0)


def key_positions():
    sq = lax.axis_index("seq")
    return (192 * sq + lax.broadcasted_iota(jnp.int32, (192, 128), 0)).astype(F32)


def ffn_place(B, C):
    def place(n, at):
        if n < 2:
            return B.at[at["x"], at["y"], at["z"], at["c"], n]
        return C.at[at["z"], at["c"], at["x"], at["y"]]
    return place


def cross_fwd_kernel(q, lens, blkB, blkC, mem_h, A, q_h, k_h, v_h, kt_h, B, C, o_ref, L_ref,
                     qall, mem, wk, wv, wkT, wvT, K, V, KT, VT, ost, lst, orc, lrc, acc,
                     mem_s, w_s, out_s, ss, rs, os_, or_, ls_, lr_, fs, fr, fsib_s, fsib_r, own_s):
    me = where_am_i()
    bar, count = meet(me, "z")

    def load_mem(e):
        return pltpu.make_async_copy(mem_h.at[e], mem.at[e], mem_s.at[e])

    loads = [pltpu.make_async_copy(A.at[10 + i], (wk if i < 2 else wv).at[:, pl.ds(384 * (i % 2), 384)], w_s.at[i]) for i in range(4)]
    for c in loads:
        c.start()

    @pl.loop(0, 16)
    def _(e):
        load_mem(e).start()

    qall[me["x"], me["y"]] = q[...]
    place = ffn_place(B, C)
    mine = lambda n: blkB.at[n] if n < 2 else blkC
    owns = [pltpu.make_async_copy(mine(n), place(n, me), own_s.at[n]) for n in range(3)]
    for c in owns:
        c.start()
    pl.semaphore_wait(bar, count)
    plane = Gather(me, ("xy", "yx"), lambda n, at: qall.at[at["x"], at["y"], :, pl.ds(384 * n, 384)],
                   lambda n: qall.at[me["x"], me["y"], :, pl.ds(384 * n, 384)], ss, rs)
    ring = Gather(me, [p[2] for p in PARTS_F], place, mine, fs, fr, fsib_s, fsib_r)
    plane.send(0)
    ring.send(0)
    for c in loads:
        c.wait()
    for i in range(6):
        wkT[:, 128 * i:128 * i + 128] = wk[128 * i:128 * i + 128, :].T
        wvT[:, 128 * i:128 * i + 128] = wv[128 * i:128 * i + 128, :].T
    plane.forward(0)
    ring.forward(0)
    for c in owns:
        c.wait()

    def project(a, b):
        @pl.loop(a, b)
        def _(e):
            load_mem(e).wait()
            m = mem[e]
            K[e] = dot(m, wk[...]).astype(BF)
            VT[e] = dot(wvT[...], m, 1, 1).astype(BF)
            V[e] = dot(m, wv[...]).astype(BF)
            KT[e] = dot(wkT[...], m, 1, 1).astype(BF)

    project(0, 3)
    plane.send(1)
    ring.send(1)
    project(3, 8)
    ring.forward(1)
    project(8, 11)
    ring.send(2)
    plane.forward(1)
    project(11, 16)
    outs = [pltpu.make_async_copy(a, b, out_s.at[i]) for i, (a, b) in enumerate(((K, k_h), (V, v_h), (KT, kt_h), (qall, q_h)))]
    for c in outs[:3]:
        c.start()
    plane.finish()
    outs[3].start()
    masks = head_masks()
    pos = key_positions()

    def o_copy(j):
        return remote(ost.at[j], orc.at[j], os_.at[j], or_.at[j], offset(me, j))

    def l_copy(j):
        return remote(lst.at[j], lrc.at[j], ls_.at[j], lr_.at[j], offset(me, j))

    def attend(a, b):
        @pl.loop(a, b)
        def _(i):
            j = (i + 1) % 16
            at = offset(me, j)
            e = at["x"] * 4 + at["y"]
            live = pos < lens[pl.ds(e, 1), :]
            for g in range(3):
                cols = slice(256 * g, 256 * g + 256)
                sT = dot(K[e, :, cols], stack_heads(qall[at["x"], at["y"], :, cols], masks), 1, 1)
                ps, inv = [], []
                for h in range(4):
                    s = jnp.where(live, sT[:, 128 * h:128 * h + 128], NEG)
                    top = jnp.max(s, axis=0, keepdims=True)
                    p = jnp.exp(s - top)
                    tot = jnp.sum(p, axis=0, keepdims=True)
                    lst[j, 4 * g + h:4 * g + h + 1, :] = top + jnp.log(tot)
                    ps.append(p.astype(BF))
                    inv.append(1.0 / tot)
                oT = dot(VT[e, cols, :], jnp.concatenate(ps, axis=1))
                for h in range(4):
                    ost[j, 256 * g + 64 * h:256 * g + 64 * h + 64, :] = (oT[64 * h:64 * h + 64, 128 * h:128 * h + 128] * inv[h]).astype(BF)

            @pl.when(j > 0)
            def _():
                l_copy(j).start()
                o_copy(j).start()

    attend(0, 8)
    ring.forward(2)
    attend(8, 16)
    lrc[0] = lst[0]
    orc[0] = ost[0]
    ring.finish()

    @pl.loop(1, 16)
    def _(j):
        l_copy(j).wait_recv()

    l = lrc[:, 0:12, :]
    top = jnp.max(l, axis=0)
    L_ref[0:12, :] = top + jnp.log(jnp.sum(jnp.exp(l - top[None]), axis=0))
    L_ref[12:16, :] = jnp.zeros((4, 128), F32)
    acc[...] = jnp.zeros_like(acc)

    @pl.loop(0, 16)
    def _(j):
        @pl.when(j > 0)
        def _():
            o_copy(j).wait_recv()

        w = jnp.exp(lrc[j, 0:12, :] - L_ref[0:12, :])
        for h in range(12):
            acc[64 * h:64 * h + 64, :] += orc[j, 64 * h:64 * h + 64, :].astype(F32) * w[h:h + 1, :]

    for i in range(6):
        o_ref[:, 128 * i:128 * i + 128] = acc[128 * i:128 * i + 128, :].T

    @pl.loop(1, 16)
    def _(j):
        l_copy(j).wait_send()
        o_copy(j).wait_send()

    plane.drain()
    for c in outs:
        c.wait()
    ring.siblings_in()
    ring.drain()


def cross_fwd(q, lens, blkB, blkC, memory, A):
    return pl.pallas_call(
        cross_fwd_kernel,
        out_shape=(SDS((4, 4, 128, 768), BF), SDS((16, 192, 768), BF), SDS((16, 192, 768), BF), SDS((16, 768, 192), BF),
                   SDS((4, 4, 4, 2, 2, 48, 256), BF), SDS((4, 2, 4, 4, 16, 768), BF), SDS((128, 768), F32), SDS((16, 128), F32)),
        in_specs=[VS] * 4 + [HS] * 2, out_specs=(HS,) * 6 + (VS,) * 2,
        scratch_shapes=[vm(4, 4, 128, 768), vm(16, 192, 768), vm(768, 768), vm(768, 768), vm(768, 768), vm(768, 768),
                        vm(16, 192, 768), vm(16, 192, 768), vm(16, 768, 192), vm(16, 768, 192), vm(16, 768, 128), vf(16, 16, 128),
                        vm(16, 768, 128), vf(16, 16, 128), vf(768, 128),
                        DMA((16,)), DMA((4,)), DMA((4,)), DMA((2, 2, 4)), DMA((2, 2, 4)), DMA((16,)), DMA((16,)), DMA((16,)), DMA((16,)),
                        DMA((3, 3, 4)), DMA((3, 3, 4)), DMA((3, 4)), DMA((3, 4)), DMA((3,))],
        compiler_params=pltpu.CompilerParams(collective_id=2, has_side_effects=True, vmem_limit_bytes=60 << 20),
        name="cross_forward",
    )(q, lens, blkB, blkC, memory, A)


def cross_bwd_kernel(do, st, lens, q_h, k_h, v_h, kt_h, mem_h, A, GB, GC, G_in, dq_ref, fB, fC, gm_h, dw_h,
                     qall, doall, stall, wk, wv, K, V, KT, mem, memT, dK, dV, gst, wst, dst, dh1, df1, dh0, df0,
                     accB, accC, sibB, sibC, hB2, hC2, fB2, fC2, hB1, hC1, fB1, fC1, hB0, hC0, fB0, fC0,
                     q_s, kv_s, mem_s, w_s, gm_s, dw_s, ss, rs, ds_, dr_, fs, fr, fsib_s, fsib_r, floc):
    me = where_am_i()
    bar, count = meet(me, "z")

    def load_mem(e):
        return pltpu.make_async_copy(mem_h.at[pl.ds(pl.multiple_of(256 * e, 256), 256)], mem.at[e % 2], mem_s.at[e % 2])

    load_mem(0).start()
    load_mem(1).start()
    loads = [pltpu.make_async_copy(A.at[10 + i], (wk if i < 2 else wv).at[:, pl.ds(384 * (i % 2), 384)], w_s.at[i]) for i in range(4)]
    loads.append(pltpu.make_async_copy(q_h, qall, q_s))
    doall[me["x"], me["y"]] = do[...]
    stall[me["x"], me["y"]] = st[...]
    pl.semaphore_wait(bar, count)

    def place(n, at):
        return stall.at[at["x"], at["y"]] if n == 2 else doall.at[at["x"], at["y"], :, pl.ds(384 * n, 384)]

    plane = Gather(me, ("xy", "yx", "xy"), place, lambda n: place(n, me), ss, rs)
    fhop, ffin = staged("BC", (hB2, hC2, fB2, fC2, hB1, hC1, fB1, fC1, hB0, hC0, fB0, fC0))
    grads = ffn_place(GB, GC)
    ring = Scatter(me, PARTS_F, {"B": accB, "C": accC}, fhop, ffin, fs, fr, {"B": sibB, "C": sibC},
                   lambda n, at, c: grads(n, {**at, "c": c}), fsib_s, fsib_r, floc)
    back = Scatter(me, PARTS_D, {"D": dst}, {1: {"D": dh1}, 0: {"D": dh0}}, {1: {"D": df1}, 0: {"D": df0}}, ds_, dr_)
    plane.send(0)
    ring.start()
    for c in loads:
        c.start()

    def turn(a, b):
        @pl.loop(a, b)
        def _(e):
            load_mem(e).wait()
            memT[:, pl.ds(pl.multiple_of(256 * e, 256), 256)] = mem[e % 2].T

            @pl.when(e < 10)
            def _():
                load_mem(e + 2).start()

    turn(0, 2)
    plane.forward(0)
    ring.merge(0)
    ring.hop(2)
    plane.send(1)
    turn(2, 7)
    ring.merge(1)
    ring.merge(2)
    plane.forward(1)
    ring.pass_on(2)
    turn(7, 12)
    ring.merge(3)
    masks = head_masks()
    pos = key_positions()

    def where(i):
        return {**me, "x": (me["x"] + 2 + i // 4) % 4, "y": (me["y"] + 2 + i % 4) % 4}

    def load_kv(i, which):
        at = where(i)
        e = at["x"] * 4 + at["y"]
        src, to = ((k_h, K), (v_h, V), (kt_h, KT))[which]
        return pltpu.make_async_copy(src.at[e], to.at[i % 2], kv_s.at[which, i % 2])

    for w in range(3):
        load_kv(0, w).start()
    for c in loads:
        c.wait()
    plane.finish()

    @pl.loop(0, 16)
    def _(i):
        at = where(i)
        e = at["x"] * 4 + at["y"]

        @pl.when(i < 15)
        def _():
            for w in range(3):
                load_kv(i + 1, w).start()

        for w in range(3):
            load_kv(i, w).wait()
        live = pos < lens[pl.ds(e, 1), :]
        rows = pl.ds(pl.multiple_of(192 * e, 192), 192)
        for g in range(3):
            cols = slice(256 * g, 256 * g + 256)
            q4s = stack_heads(qall[at["x"], at["y"], :, cols], masks)
            d4s = stack_heads(doall[at["x"], at["y"], :, cols], masks)
            sT = dot(K[i % 2, :, cols], q4s, 1, 1)
            gT = dot(V[i % 2, :, cols], d4s, 1, 1)
            ps, gs = [], []
            for h in range(4):
                n = 4 * g + h
                s = jnp.where(live, sT[:, 128 * h:128 * h + 128], NEG)
                p = jnp.exp(s - stall[at["x"], at["y"], n:n + 1, :])
                ps.append(p.astype(BF))
                gs.append((p * (gT[:, 128 * h:128 * h + 128] - stall[at["x"], at["y"], 12 + n:13 + n, :])).astype(BF))
            sg = jnp.concatenate(gs, axis=1)
            dV[rows, cols] = dot(jnp.concatenate(ps, axis=1), d4s).astype(BF)
            dK[rows, cols] = dot(sg, q4s).astype(BF)
            qT = dot(KT[i % 2, cols, :], sg)
            for h in range(4):
                r = 256 * g + 64 * h
                dst[r // 384, at["x"], at["y"], r % 384:r % 384 + 64, :] = qT[64 * h:64 * h + 64, 128 * h:128 * h + 128].astype(BF)

    back.hop(1)

    def gm_copy(e):
        return pltpu.make_async_copy(gst.at[e % 2], gm_h.at[e], gm_s.at[e % 2])

    def mem_grad(a, b):
        @pl.loop(a, b)
        def _(e):
            @pl.when(e > 1)
            def _():
                gm_copy(e - 2).wait()

            rows = pl.ds(pl.multiple_of(192 * e, 192), 192)
            gst[e % 2] = dot(dK[rows, :], wk[...], 1, 1) + dot(dV[rows, :], wv[...], 1, 1)
            gm_copy(e).start()

    def dw_copy(n, r):
        return pltpu.make_async_copy(wst.at[n % 2], dw_h.at[10 + n, pl.ds(pl.multiple_of(128 * r, 128), 128)], dw_s.at[n % 2])

    def weight_grad(n):
        src = dK if n < 2 else dV

        @pl.loop(0, 6)
        def _(r):
            @pl.when(r > 0)
            def _():
                dw_copy(n, r - 1).wait()

            wst[n % 2] = dot(memT[pl.ds(pl.multiple_of(128 * r, 128), 128), :], src[:, 384 * (n % 2):384 * (n % 2) + 384]).astype(BF)
            dw_copy(n, r).start()

        dw_copy(n, 5).wait()

    mem_grad(0, 5)
    back.pass_on(1)
    ring.close(2)
    ring.hop(1)
    mem_grad(5, 16)
    ring.pass_on(1)
    weight_grad(0)
    back.close(1)
    back.hop(0)
    ring.close(1)
    ring.hop(0)
    weight_grad(1)
    back.pass_on(0)
    ring.pass_on(0)
    weight_grad(2)
    weight_grad(3)
    for n in range(2):
        v = 0.125 * back.result(n)
        for i in range(3):
            dq_ref[:, 384 * n + 128 * i:384 * n + 128 * i + 128] = v[128 * i:128 * i + 128, :].T
    fB[0:48, :] = ring.result(0)
    fB[48:96, :] = ring.result(1)
    fC[...] = ring.result(2)
    gm_copy(14).wait()
    gm_copy(15).wait()
    plane.drain()
    ring.drain()
    back.drain()


def cross_bwd(do, st, lens, q_h, k_h, v_h, kt_h, memory, A, GB, GC, GA):
    bB, bC = (48, 256), (16, 768)
    return pl.pallas_call(
        cross_bwd_kernel,
        out_shape=(SDS((128, 768), F32), SDS((96, 256), F32), SDS((16, 768), F32), SDS((16, 192, 768), F32), SDS((16, 768, 384), BF)),
        in_specs=[VS] * 3 + [HS] * 9, out_specs=(VS,) * 3 + (HS,) * 2, input_output_aliases={11: 4},
        scratch_shapes=[vm(4, 4, 128, 768), vm(4, 4, 128, 768), vf(4, 4, 24, 128), vm(768, 768), vm(768, 768),
                        vm(2, 192, 768), vm(2, 192, 768), vm(2, 768, 192), vm(2, 256, 768), vm(768, 3072), vm(3072, 768), vm(3072, 768),
                        vf(2, 192, 768), vm(2, 128, 384), vm(2, 4, 4, 384, 128), vm(2, 2, 2, 384, 128), vm(2, 2, 4, 384, 128), vm(2, 2, 384, 128), vm(2, 2, 384, 128),
                        vm(2, 4, 4, 4, *bB), vm(4, 4, 4, *bC), vm(2, 4, 4, 4, *bB), vm(4, 4, 4, *bC), *stage_buffers(((2,), bB), ((), bC)),
                        DMA, DMA((3, 2)), DMA((2,)), DMA((4,)), DMA((2,)), DMA((2,)), DMA((3, 2, 4)), DMA((3, 2, 4)), DMA((2, 2, 4)), DMA((2, 2, 4)),
                        DMA((3, 3, 4)), DMA((3, 3, 4)), DMA((3, 4)), DMA((3, 4)), DMA((3, 4))],
        compiler_params=pltpu.CompilerParams(collective_id=3, has_side_effects=True, vmem_limit_bytes=60 << 20),
        name="cross_backward",
    )(do, st, lens, q_h, k_h, v_h, kt_h, memory.reshape(3072, 768), A, GB, GC, GA)


def adam_update(master, first, second, grad, rate):
    first_new = beta_one * first + (1.0 - beta_one) * grad
    second_new = beta_two * second + (1.0 - beta_two) * grad * grad
    fix_one = 1.0 - beta_one**STEP
    fix_two = 1.0 - beta_two**STEP
    master_new = master - rate * (
        first_new / fix_one / (jnp.sqrt(second_new / fix_two) + adam_eps) + decay_rate * master
    )
    return (master_new, first_new, second_new, master_new.astype(jnp.bfloat16))


def rms(x):
    return lax.rsqrt(jnp.mean(x * x, axis=-1, keepdims=True) + eps_norm)

def rms_back(x, inv, gain, u):
    scaled = u * gain
    inner = jnp.mean(scaled * x, axis=-1, keepdims=True)
    return inv * scaled - x * inv * inv * inv * inner, jnp.sum(u * x * inv, axis=0, keepdims=True)

def flip(x):
    return jnp.concatenate([x[:, 128 * i:128 * i + 128].T for i in range(x.shape[1] // 128)], axis=0)

def unflip(x):
    return jnp.concatenate([x[128 * i:128 * i + 128, :].T for i in range(x.shape[0] // 128)], axis=1)

def apply_w(h, W, k):
    return jnp.concatenate([dot(h, W[2 * k]), dot(h, W[2 * k + 1])], axis=1)

def apply_wt(u, W, k):
    return dot(u[:, 0:384], W[2 * k], 1, 1) + dot(u[:, 384:768], W[2 * k + 1], 1, 1)

def causal_mask():
    return lax.broadcasted_iota(jnp.int32, (128, 128), 0) <= lax.broadcasted_iota(jnp.int32, (128, 128), 1)

def self_fwd_kernel(x_ref, gains, A, q2, h1, qkv, o1, x1, h2, L1, W, sem):
    loads = [pltpu.make_async_copy(A.at[i], W.at[i], sem.at[i]) for i in range(10)]
    for c in loads:
        c.start()
    x = x_ref[...].astype(F32)
    h = (x * rms(x) * gains[0:1, :]).astype(BF)
    h1[...] = h
    for k in range(3):
        loads[2 * k].wait()
        loads[2 * k + 1].wait()
        full = apply_w(h, W, k)
        qkv[k] = full.astype(BF)
    vT = flip(full).astype(BF)
    masks = head_masks(0.125)
    live = causal_mask()
    outs = []
    for g in range(3):
        cols = slice(256 * g, 256 * g + 256)
        q4 = qkv[0, :, cols]
        sT = dot(qkv[1, :, cols], jnp.concatenate([q4 * m for m in masks], axis=0), 1, 1)
        ps = []
        for n in range(4):
            s = jnp.where(live, sT[:, 128 * n:128 * n + 128], NEG)
            top = jnp.max(s, axis=0, keepdims=True)
            lse = top + jnp.log(jnp.sum(jnp.exp(s - top), axis=0, keepdims=True))
            L1[4 * g + n:4 * g + n + 1, :] = lse
            ps.append(jnp.exp(s - lse).astype(BF))
        oT = dot(vT[256 * g:256 * g + 256, :], jnp.concatenate(ps, axis=1))
        outs += [oT[64 * n:64 * n + 64, 128 * n:128 * n + 128] for n in range(4)]
    o = unflip(jnp.concatenate(outs, axis=0)).astype(BF)
    o1[...] = o
    for c in loads[6:]:
        c.wait()
    x = x + apply_w(o, W, 3)
    x1[...] = x
    h = (x * rms(x) * gains[1:2, :]).astype(BF)
    h2[...] = h
    q2[...] = apply_w(h, W, 4).astype(BF) * jnp.asarray(0.125, BF)

def self_fwd(x, gains, A):
    row = SDS((128, 768), BF)
    return pl.pallas_call(
        self_fwd_kernel,
        out_shape=(row, row, SDS((3, 128, 768), BF), row, SDS((128, 768), F32), row, SDS((16, 128), F32)),
        in_specs=[VS, VS, HS], out_specs=(VS,) * 7,
        scratch_shapes=[pltpu.VMEM((10, 768, 384), BF), pltpu.SemaphoreType.DMA((10,))],
        compiler_params=pltpu.CompilerParams(vmem_limit_bytes=60 << 20),
        name="self_forward",
    )(x, gains, A)

def ffn_kernel(x1, o2, L2, dy_ref, gains, A, B, C, out, do2, st, dx2, gg, GA, GB, GC,
               W7, WB, WC, gA, gB, gC, sw, sb, sc, tb, tc, ta):
    lA = [pltpu.make_async_copy(A.at[14 + i], W7.at[i], sw.at[i]) for i in range(2)]
    lB = [pltpu.make_async_copy(B.at[i], WB.at[i], sb.at[i]) for i in range(16)]
    lC = [pltpu.make_async_copy(C.at[i], WC.at[i], sc.at[i]) for i in range(8)]
    for c in lA:
        c.start()
    for j in range(8):
        lB[j].start()
        lB[8 + j].start()
        lC[j].start()
    o = o2[...]
    ob = o.astype(BF)
    for c in lA:
        c.wait()
    x = x1[...] + apply_w(ob, W7, 0)
    inv = rms(x)
    h = (x * inv * gains[2:3, :]).astype(BF)
    hT = flip(h.astype(F32)).astype(BF)
    df = dy_ref[...]
    y = jnp.zeros((128, 768), F32)
    dh = jnp.zeros((128, 768), F32)
    c0 = 0.7978845608028654
    sB, sC = [], []
    for j in range(8):
        lB[j].wait()
        lB[8 + j].wait()
        lC[j].wait()
        a = dot(h, WB[j])
        up = dot(h, WB[8 + j])
        t = jnp.tanh(c0 * (a + 0.044715 * a * a * a))
        half = 0.5 * (1.0 + t)
        gel = a * half
        der = half + 0.5 * a * (1.0 - t * t) * (c0 * (1.0 + 0.134145 * a * a))
        mid32 = gel * up
        mid = mid32.astype(BF)
        y += dot(mid, WC[j])
        dm = dot(df, WC[j], 1, 1)
        dga = (dm * up * der).astype(BF)
        dup = (dm * gel).astype(BF)
        dh += dot(dga, WB[j], 1, 1) + dot(dup, WB[8 + j], 1, 1)
        gB[j] = dot(hT, dga).astype(BF)
        gB[8 + j] = dot(hT, dup).astype(BF)
        gC[j] = dot(flip(mid32).astype(BF), df).astype(BF)
        sB += [pltpu.make_async_copy(gB.at[j], GB.at[j], tb.at[j]), pltpu.make_async_copy(gB.at[8 + j], GB.at[8 + j], tb.at[8 + j])]
        sC += [pltpu.make_async_copy(gC.at[j], GC.at[j], tc.at[j])]
        for c in sB[-2:] + sC[-1:]:
            c.start()
    out[...] = (x + y).astype(BF)
    dz, gain = rms_back(x, inv, gains[2:3, :], dh)
    gg[...] = gain
    d = df.astype(F32) + dz
    dx2[...] = d
    dc = d.astype(BF)
    dof = apply_wt(dc, W7, 0).astype(BF)
    do2[...] = dof
    prod = flip(dof.astype(F32) * o)
    st[0:12, :] = L2[0:12, :]
    for n in range(12):
        st[12 + n:13 + n, :] = jnp.sum(prod[64 * n:64 * n + 64, :], axis=0, keepdims=True)
    oT = flip(o).astype(BF)
    sA = []
    for i in range(2):
        gA[i] = dot(oT, dc[:, 384 * i:384 * i + 384]).astype(BF)
        sA.append(pltpu.make_async_copy(gA.at[i], GA.at[14 + i], ta.at[i]))
        sA[-1].start()
    for c in sA + sB + sC:
        c.wait()

def ffn(x1, o2, L2, dy, gains, A, B, C):
    M = lambda *s: pltpu.VMEM(s, BF)
    D = pltpu.SemaphoreType.DMA
    return pl.pallas_call(
        ffn_kernel,
        out_shape=(SDS((128, 768), BF), SDS((128, 768), BF), SDS((24, 128), F32), SDS((128, 768), F32), SDS((1, 768), F32),
                   SDS((16, 768, 384), BF), SDS((16, 768, 256), BF), SDS((8, 256, 768), BF)),
        in_specs=[VS] * 5 + [HS] * 3, out_specs=(VS,) * 5 + (HS,) * 3,
        scratch_shapes=[M(2, 768, 384), M(16, 768, 256), M(8, 256, 768), M(2, 768, 384), M(16, 768, 256), M(8, 256, 768),
                        D((2,)), D((16,)), D((8,)), D((16,)), D((8,)), D((2,))],
        compiler_params=pltpu.CompilerParams(vmem_limit_bytes=60 << 20),
        name="feed_forward",
    )(x1, o2, L2, dy, gains, A, B, C)

def self_bwd_kernel(dq2, h2, x1, dx2, qkv, o1, L1, x_ref, h1, gains, g3, A, GA_in, gm_in, gin, tile, GA, gm,
                    W, G, gb, gmv, sem, gsem, msem):
    loads = [pltpu.make_async_copy(A.at[i], W.at[i], sem.at[i]) for i in range(10)]
    for i in (8, 9, 6, 7, 0, 1, 2, 3, 4, 5):
        loads[i].start()
    def gm_load(e):
        return pltpu.make_async_copy(gm_in.at[e], gmv.at[e], msem.at[e])
    def gm_store(e):
        return pltpu.make_async_copy(gmv.at[e], gm.at[e], msem.at[16 + e])
    for e in range(16):
        gm_load(e).start()
    stores = []
    def weight_grad(k, left, inc):
        for i in range(2):
            n = 2 * k + i
            G[n] = dot(left, inc[:, 384 * i:384 * i + 384]).astype(BF)
            stores.append(pltpu.make_async_copy(G.at[n], GA.at[n], gsem.at[n]))
            stores[-1].start()
    dqb = dq2[...].astype(BF)
    for i in (8, 9, 6, 7):
        loads[i].wait()
    u = apply_wt(dqb, W, 4)
    x = x1[...]
    inv = rms(x)
    dz, gain = rms_back(x, inv, gains[1:2, :], u)
    gb[...] = jnp.zeros((8, 768), F32)
    gb[1:2, :] = gain
    gb[2:3, :] = g3[...]
    d1 = dx2[...] + dz
    da = d1.astype(BF)
    do1 = apply_wt(da, W, 3).astype(BF)
    weight_grad(4, flip(h2[...].astype(F32)).astype(BF), dqb)
    masks = head_masks(0.125)
    ones = head_masks(1.0)
    live = causal_mask()
    kT = flip(qkv[1].astype(F32)).astype(BF)
    qs, ks, vs = [], [], []
    for g in range(3):
        cols = slice(256 * g, 256 * g + 256)
        q4 = qkv[0, :, cols]
        d4 = do1[:, cols]
        q4s = jnp.concatenate([q4 * m for m in masks], axis=0)
        d4s = jnp.concatenate([d4 * m for m in ones], axis=0)
        sT = dot(qkv[1, :, cols], q4s, 1, 1)
        gT = dot(qkv[2, :, cols], d4s, 1, 1)
        ps, gs = [], []
        for n in range(4):
            s = jnp.where(live, sT[:, 128 * n:128 * n + 128], NEG)
            p = jnp.exp(s - L1[4 * g + n:4 * g + n + 1, :])
            gt = gT[:, 128 * n:128 * n + 128]
            ps.append(p.astype(BF))
            gs.append((p * (gt - jnp.sum(p * gt, axis=0, keepdims=True))).astype(BF))
        sg = jnp.concatenate(gs, axis=1)
        vs.append(dot(jnp.concatenate(ps, axis=1), d4s).astype(BF))
        ks.append(dot(sg, q4s).astype(BF))
        qT = dot(kT[256 * g:256 * g + 256, :], sg)
        qs += [qT[64 * n:64 * n + 64, 128 * n:128 * n + 128] for n in range(4)]
    for e in range(16):
        gm_load(e).wait()
        gm_store(e).start()
    inc = [(0.125 * unflip(jnp.concatenate(qs, axis=0))).astype(BF), jnp.concatenate(ks, axis=1), jnp.concatenate(vs, axis=1)]
    weight_grad(3, flip(o1[...].astype(F32)).astype(BF), da)
    for c in loads[:6]:
        c.wait()
    u = apply_wt(inc[0], W, 0) + apply_wt(inc[1], W, 1) + apply_wt(inc[2], W, 2)
    x = x_ref[...].astype(F32)
    inv = rms(x)
    dz, gain = rms_back(x, inv, gains[0:1, :], u)
    gb[0:1, :] = gain
    gin[...] = d1 + dz
    hT = flip(h1[...].astype(F32)).astype(BF)
    for k in range(3):
        weight_grad(k, hT, inc[k])
    lane = lax.broadcasted_iota(jnp.int32, (8, 128), 1)
    for d in range(8):
        lo, sh = 96 * d // 128, 96 * d % 128
        t = pltpu.roll(gb[:, 128 * lo:128 * lo + 128], (128 - sh) % 128, 1)
        if sh > 32:
            nxt = pltpu.roll(gb[:, 128 * lo + 128:128 * lo + 256], (128 - sh) % 128, 1)
            t = jnp.where(lane < 128 - sh, t, nxt)
        tile[d] = jnp.where(lane < 96, t, 0.0)
    for c in stores:
        c.wait()
    for e in range(16):
        gm_store(e).wait()

def self_bwd(dq2, h2, x1, dx2, qkv, o1, L1, x, h1, gains, g3, A, GA, gm):
    D = pltpu.SemaphoreType.DMA
    return pl.pallas_call(
        self_bwd_kernel,
        out_shape=(SDS((128, 768), F32), SDS((8, 8, 128), F32), SDS((16, 768, 384), BF), SDS((16, 192, 768), F32)),
        in_specs=[VS] * 11 + [HS] * 3, out_specs=(VS, VS, HS, HS),
        input_output_aliases={12: 2},
        scratch_shapes=[pltpu.VMEM((10, 768, 384), BF), pltpu.VMEM((10, 768, 384), BF), pltpu.VMEM((8, 768), F32), pltpu.VMEM((16, 192, 768), F32), D((10,)), D((10,)), D((32,))],
        compiler_params=pltpu.CompilerParams(vmem_limit_bytes=60 << 20),
        name="self_backward",
    )(dq2, h2, x1, dx2, qkv, o1, L1, x, h1, gains, g3, A, GA, gm)

def adam_kernel(*refs):
    ins, outs = refs[:16], refs[16:]
    for n in range(4):
        w, m, v, g = ins[4 * n:4 * n + 4]
        grad = g[0:3, 0:6] if n == 3 else g[...]
        for o, val in zip(outs[4 * n:4 * n + 4], adam_update(w[...], m[...], v[...], grad, rate_gain if n == 3 else rate_matrix)):
            o[...] = val

def adam(*args):
    shapes = []
    for n in range(4):
        s = args[4 * n].shape
        shapes += [SDS(s, F32)] * 3 + [SDS(s, BF)]
    return pl.pallas_call(adam_kernel, out_shape=tuple(shapes), in_specs=[VS] * 16, out_specs=(VS,) * 16,
                          compiler_params=pltpu.CompilerParams(vmem_limit_bytes=60 << 20), name="adam")(*args)


def body(
    dec_input,
    memory,
    mem_len,
    grad_out,
    attn_master,
    ffn_in_master,
    ffn_out_master,
    gain_master,
    attn_first,
    ffn_in_first,
    ffn_out_first,
    gain_first,
    attn_second,
    ffn_in_second,
    ffn_out_second,
    gain_second,
):
    swap = lambda a: a.transpose(1, 0, 2)
    attn_t, in_t = swap(attn_master), swap(ffn_in_master)
    gath_a, gains, lens, blk_b, blk_c = gather(attn_t, in_t, ffn_out_master, info_tile(gain_master, mem_len))
    aw = gath_a.reshape(16, 768, 384)
    x = dec_input[0]
    q2, h1, qkv, o1, x1, h2, L1 = self_fwd(x, gains, aw)
    q_all, k_two, v_two, kt_two, gath_b, gath_c, o2, L2 = cross_fwd(q2, lens, blk_b, blk_c, memory, aw)
    out_block, do2, st, dx2, g3, GA, GB, GC = ffn(x1, o2, L2, grad_out[0], gains, aw, gath_b.reshape(16, 768, 256), gath_c.reshape(8, 256, 768))
    dq2, blk_f, share_c, gm, GA = cross_bwd(
        do2, st, lens, q_all, k_two, v_two, kt_two, memory, aw,
        GB.reshape(4, 4, 4, 2, 2, 48, 256), GC.reshape(4, 2, 4, 4, 16, 768), GA,
    )
    grad_input, tile_g, GA, grad_memory = self_bwd(dq2, h2, x1, dx2, qkv, o1, L1, x, h1, gains, g3, aw, GA, gm)
    share_a, share_b, share_g = scatter(GA.reshape(4, 4, 4, 2, 3, 32, 384), blk_f, tile_g)
    new = adam(
        attn_t, swap(attn_first), swap(attn_second), share_a,
        in_t, swap(ffn_in_first), swap(ffn_in_second), share_b,
        ffn_out_master, ffn_out_first, ffn_out_second, share_c,
        gain_master, gain_first, gain_second, share_g,
    )
    return (out_block[None], grad_input[None], grad_memory, *[swap(a) for a in new[:8]], *new[8:])


def solution(mesh):
    placed = (
        P(("dp", "seq"), None, None),
        P("dp", "seq", None),
        P(("dp", "seq")),
        P(("dp", "seq"), None, None),
        P(None, ("dp", "seq"), None),
        P(None, ("dp", "seq"), None),
        P(("dp", "seq"), None),
        P(None, ("dp", "seq")),
        P(None, ("dp", "seq"), None),
        P(None, ("dp", "seq"), None),
        P(("dp", "seq"), None),
        P(None, ("dp", "seq")),
        P(None, ("dp", "seq"), None),
        P(None, ("dp", "seq"), None),
        P(("dp", "seq"), None),
        P(None, ("dp", "seq")),
    )
    return jax.shard_map(
        body,
        mesh=mesh,
        in_specs=placed,
        out_specs=(
            P(("dp", "seq"), None, None),
            P(("dp", "seq"), None, None),
            P("dp", "seq", None),
            P(None, ("dp", "seq"), None),
            P(None, ("dp", "seq"), None),
            P(None, ("dp", "seq"), None),
            P(None, ("dp", "seq"), None),
            P(None, ("dp", "seq"), None),
            P(None, ("dp", "seq"), None),
            P(None, ("dp", "seq"), None),
            P(None, ("dp", "seq"), None),
            P(("dp", "seq"), None),
            P(("dp", "seq"), None),
            P(("dp", "seq"), None),
            P(("dp", "seq"), None),
            P(None, ("dp", "seq")),
            P(None, ("dp", "seq")),
            P(None, ("dp", "seq")),
            P(None, ("dp", "seq")),
        ),
        check_vma=False,
    )
```

time: 355 us -> 351 us (0.989); the launches traced: 355 us -> 346 us
  Pallas kernels: 352 us -> 343 us
    pallas_call x4, Pallas kernels: 310 us -> 301 us  [the longest x1 104 us: cross_bwd(): pl.pallas_call(cross_bwd_kernel, out_shape=(SDS((128, 768), F32), SDS((96...]
where the time goes in v1:
time: 351 us; the launch traced here: 346 us
  Pallas kernels  343 us (98%)
    pallas_call x1, Pallas kernels, cross_bwd(): pl.pallas_call(cross_bwd_kernel, out_shape=(SDS((128, 768), F32), SDS((96...  104 us
    pallas_call x1, Pallas kernels, cross_fwd(): pl.pallas_call(cross_fwd_kernel, out_shape=(SDS((4, 4, 128, 768), BF), SD...  95.8 us
    pallas_call x1, Pallas kernels, gather(): pl.pallas_call(gather_kernel, out_shape=(SDS((4, 4, 4, 2, 3, 32, 384), BF...  51.8 us
    pallas_call x1, Pallas kernels, scatter(): pl.pallas_call(scatter_kernel, out_shape=(SDS((6, 8, 768), F32), SDS((6,...  50.1 us
    pallas_call x1, Pallas kernels, ffn(): pl.pallas_call(ffn_kernel, out_shape=(SDS((128, 768), BF), SDS((128, 768)...  19.3 us
    pallas_call x1, Pallas kernels, self_bwd(): pl.pallas_call(self_bwd_kernel, out_shape=(SDS((128, 768), F32), SDS((8,...  13.7 us

profile of v1, /device:TPU:0, one launch (start us, length us, event | category | flops | bytes accessed | tf_op | source)
XLA Modules:
  0.0 346.1 jit_solution(885296225790303376)
XLA Ops:
  1.3 0.7 convert_convert_fusion
  2.0 0.2 dynamic_update_slice.6
  2.2 0.1 dynamic_update_slice.7.info
  2.3 0.0 copy-start
  2.3 0.6 copy-done
  2.9 51.8 %gather_attention_weights.1 = (bf16[4,4,4,2,3,32,384]{6,5,4,3,2,1,0:T(8,128)(2,1)}, f32[8,768]{1,0:T(8,128)}, f32[16,128]{1,0:T(8,128)}, bf16[2,48,256]{2,1,0:T(8,128)(2,1)}, bf16[16,768]{1,0:T(8,128)(2,1)}) custom-call(f32[6,8,768]{2,1,0:T(8,128)} %bitcast.39, f32[6,2,2048]{2,1,0:T(2,128)} %bitcast.41, f32[16,768]{1,0:T(8,128)} %refs_8_.1, f32[8,128]{1,0:T(8,128)} %copy-done), custom_call_target="tpu_custom_call" | custom-call | tf_op jit(solution)/shard_map/gather_attention_weights/pallas_call | solution.py:404
  54.7 5.9 %self_forward.1 = (bf16[128,768]{1,0:T(8,128)(2,1)}, bf16[128,768]{1,0:T(8,128)(2,1)}, bf16[3,128,768]{2,1,0:T(8,128)(2,1)}, bf16[128,768]{1,0:T(8,128)(2,1)}, f...) custom-call(bf16[128,768]{1,0:T(8,128)(2,1)} %bitcast.37, f32[8,768]{1,0:T(8,128)} %get-tuple-element.75.gains, ...), custom_call_target="tpu_custom_call" | custom-call | tf_op jit(solution)/shard_map/self_forward/pallas_call | solution.py:949
  60.6 95.8 %cross_forward.1 = (bf16[4,4,128,768]{3,2,1,0:T(8,128)(2,1)}, bf16[16,192,768]{2,1,0:T(8,128)(2,1)}, bf16[16,192,768]{2,1,0:T(8,128)(2,1)}, bf16[16,768,192]{2,1...) custom-call(bf16[128,768]{1,0:T(8,128)(2,1)} %get-tuple-element.78.q, ...), custom_call_target="tpu_custom_call" | custom-call | tf_op jit(solution)/shard_map/cross_forward/pallas_call | solution.py:672
  156.4 19.3 %feed_forward.1 = (bf16[128,768]{1,0:T(8,128)(2,1)}, bf16[128,768]{1,0:T(8,128)(2,1)}, f32[24,128]{1,0:T(8,128)}, f32[128,768]{1,0:T(8,128)}, f32[1,768]{1,0:T(1...) custom-call(f32[128,768]{1,0:T(8,128)} %get-tuple-element.77.x1, ...), custom_call_target="tpu_custom_call" | custom-call | tf_op jit(solution)/shard_map/feed_forward/pallas_call | solution.py:1030
  175.8 103.6 %cross_backward.1 = (f32[128,768]{1,0:T(8,128)}, f32[96,256]{1,0:T(8,128)}, f32[16,768]{1,0:T(8,128)}, f32[16,192,768]{2,1,0:T(8,128)}, bf16[16,768,384]{2,1,0:T(8,128)(2,1)}) custom-call(bf16[128,768]{1,0:T(8,128)(2,1)} %get-tuple-element.87.do, f32[24,128]{1,0:T(8,128)} %get-tuple-element.88.st, ...), custom_call_target="tpu_custom_call", output_to_operand_aliasing={{4}: (11, {})} | custom-call | tf_op jit(solution)/shard_map/cross_backward/pallas_call | solution.py:859
  279.3 13.7 %self_backward.1 = (f32[128,768]{1,0:T(8,128)}, f32[8,8,128]{2,1,0:T(8,128)}, bf16[16,768,384]{2,1,0:T(8,128)(2,1)}, f32[16,192,768]{2,1,0:T(8,128)}) custom-call(f32[128,768]{1,0:T(8,128)} %get-tuple-element.96.dq2, bf16[128,768]{1,0:T(8,128)(2,1)} %get-tuple-element.97.h2, f32[128,768]{1,0:T(8,128)} %get-tuple-element.77.x1, ...), custom_call_target="tpu_custom_call", output_to_operand_aliasing={{2}: (12, {})} | custom-call | tf_op jit(solution)/shard_map/self_backward/pallas_call | solution.py:1129
  293.1 50.1 %scatter_attention_grads.1 = (f32[6,8,768]{2,1,0:T(8,128)}, f32[6,2,2048]{2,1,0:T(2,128)}, f32[8,128]{1,0:T(8,128)}) custom-call(bf16[4,4,4,2,3,32,384]{6,5,4,3,2,1,0:T(8,128)(2,1)} %bitcast.31, f32[96,256]{1,0:T(8,128)} %get-tuple-element.109.blkF, f32[8,8,128]{2,1,0:T(8,128)} %get-tuple-element.110.gg), custom_call_target="tpu_custom_call" | custom-call | tf_op jit(solution)/shard_map/scatter_attention_grads/pallas_call | solution.py:494
  343.2 2.5 adam.1
  (1 shorter events, 0.0 us)
Async XLA Ops:
  2.3 0.6 copy-start
